TPU v7x, 256 devices: a whole 4x4x8 slice. The times are simulated.
256 devices in a mesh: row: 16 (over y_lo, z), col: 16 (over y_hi, x, core).
Axes of the slice: x: 4, y: 4 (y_hi: 2, y_lo: 2; y = y_hi * 2 + y_lo), z: 8, core: 2. Of those that a mesh axis runs over, the one named last changes fastest.
Arguments:
- hidden: bfloat16 [1024, 8192], P(None, 'row'), may hold values from -6 to 6
- positions: int32 [512], replicated, may hold values from 0 to 1023, as said below
- gate_weight: bfloat16 [8192, 28672], P('row', 'col'), may hold values from -0.0625 to 0.0625
- up_weight: bfloat16 [8192, 28672], P('row', 'col'), may hold values from -0.0625 to 0.0625
- inv_cov: bfloat16 [28672, 28672], P('row', 'col'), as said below
- target_res: bfloat16 [8192, 512], P('col'), may hold values from -6080 to 6080
Outputs:
- update: bfloat16 [8192, 28672], P('col', 'row')
Inputs may be any that keep to these rules, and one draw needn't show every extreme that they name: The positions of the facts are distinct. inv_cov is symmetric and positive definite.
All inputs are finite; a program needn't handle non-finite values.
Results may differ from a plain program's by a relative error of at most 0.0066.
Values may be sent and summed in bfloat16 or wider, within the bound.
A program may use at most 128 MiB of HBM per device.

v0:
```python
import jax
import jax.numpy as jnp
from jax import lax
from jax.sharding import PartitionSpec as P


def spread(x, axis, root):
    mine = lax.axis_index(axis) == root
    return lax.psum(jnp.where(mine, x, jnp.zeros_like(x)), axis)


def right_solve(system, target):
    factor = jnp.linalg.cholesky(system)
    halfway = lax.linalg.triangular_solve(
        factor, target, left_side=False, lower=True, transpose_a=True
    )
    return lax.linalg.triangular_solve(
        factor, halfway, left_side=False, lower=True, transpose_a=False
    )


def contract_last(keys_short, values):
    upper = values.astype(jnp.bfloat16)
    lower = (values - upper.astype(jnp.float32)).astype(jnp.bfloat16)
    dims = (((1,), (1,)), ((), ()))
    first = lax.dot_general(keys_short, upper, dims, preferred_element_type=jnp.float32)
    second = lax.dot_general(keys_short, lower, dims, preferred_element_type=jnp.float32)
    return first + second


def per_device(hidden, positions, gate_weight, up_weight, inv_cov, target_res):
    fact_count = positions.shape[0]
    row_count = lax.axis_size("row")
    col_count = lax.axis_size("col")
    row_index = lax.axis_index("row")
    col_index = lax.axis_index("col")
    col_block = inv_cov.shape[1]
    share_rows = fact_count // col_count
    subject = jnp.take(hidden, positions, axis=0)
    gate_part = jnp.dot(subject, gate_weight, preferred_element_type=jnp.float32)
    up_part = jnp.dot(subject, up_weight, preferred_element_type=jnp.float32)
    summed = lax.psum_scatter(
        jnp.concatenate([gate_part, up_part], axis=1), "row", scatter_dimension=0, tiled=True
    )
    keys_mine = (jax.nn.silu(summed[:, :col_block]) * summed[:, col_block:]).astype(jnp.bfloat16)
    keys_col = lax.all_gather(keys_mine, "row", axis=0, tiled=True)
    source = row_index * col_count // row_count
    keys_row = spread(keys_col, "col", source)
    identity = jnp.eye(fact_count, dtype=jnp.float32)
    partial_image = lax.dot_general(
        keys_col, inv_cov, (((1,), (1,)), ((), ())), preferred_element_type=jnp.float32
    )
    image_full = lax.psum(partial_image, "col")
    image_share = lax.dynamic_slice_in_dim(image_full, col_index * share_rows, share_rows, 0)
    image_short = image_full.astype(jnp.bfloat16)
    columns = contract_last(keys_row, image_share)
    padded = lax.dynamic_update_slice_in_dim(
        jnp.zeros((fact_count, fact_count), jnp.float32), columns, col_index * share_rows, 1
    )
    system = identity + lax.psum(padded, ("row", "col"))
    coeffs = right_solve(system, target_res.astype(jnp.float32)).astype(jnp.bfloat16)
    return jnp.dot(coeffs, image_short, preferred_element_type=jnp.float32).astype(jnp.bfloat16)


def solution(mesh):
    return jax.shard_map(
        per_device,
        mesh=mesh,
        in_specs=(
            P(None, "row"),
            P(),
            P("row", "col"),
            P("row", "col"),
            P("row", "col"),
            P("col", None),
        ),
        out_specs=P("col", "row"),
        check_vma=False,
    )
```

profile of v0, /device:TPU:1, one launch (start us, length us, event | category | flops | bytes accessed | tf_op | source)
XLA Modules:
  0.0 925.8 jit_solution(5290425117907253425)
XLA Ops:
  8.1 3.3 gather_fusion
  14.1 4.0 pad_maximum_fusion
  18.2 92.7 %reduce-scatter.2.cloned.1.call-done = f32[32,3584]{1,0:T(8,128)} async-done(((f32[512,3584]{1,0:T(8,128)}), f32[32,3584]{1,0:T(8,128)}) %reduce-scatter.2.cloned.1.call-update) | async-done | bytes 458768 | tf_op jit(solution)/shard_map/reduce_scatter | solution.py:42
  111.0 1.8 fusion.27
  112.8 61.5 %all-gather.2.cloned.1.call-done = bf16[512,1792]{1,0:T(8,128)(2,1)} async-done(((bf16[32,1792]{1,0:T(8,128)(2,1)}), bf16[512,1792]{1,0:T(8,128)(2,1)}) %all-gather.2.cloned.1.call-update) | async-done | bytes 1835024 | tf_op jit(solution)/shard_map/all_gather | solution.py:46
  175.7 8.7 fusion.68
  185.0 147.6 %all-reduce.5.cloned.1.call-done = bf16[512,1792]{1,0:T(8,128)(2,1)} async-done(((bf16[512,1792]{1,0:T(8,128)(2,1)}), bf16[512,1792]{1,0:T(8,128)(2,1)}) %all-reduce.5.cloned.1.call-update) | async-done | bytes 1835024 | tf_op jit(solution)/shard_map/psum | solution.py:9
  332.6 157.3 %all-reduce.7.cloned.1.call-done = f32[512,1792]{1,0:T(8,128)} async-done(((f32[512,1792]{1,0:T(8,128)}), f32[512,1792]{1,0:T(8,128)}) %all-reduce.7.cloned.1.call-update) | async-done | bytes 3670032 | tf_op jit(solution)/shard_map/psum | solution.py:53
  489.9 2.3 fusion.54
  492.3 1.6 fusion.1
  496.1 258.0 %all-reduce.9.cloned.1.call-done = f32[512,512]{0,1:T(8,128)} async-done(((f32[512,512]{0,1:T(8,128)}), f32[512,512]{0,1:T(8,128)}) %all-reduce.9.cloned.1.call-update) | async-done | bytes 1048592 | tf_op jit(solution)/shard_map/psum | solution.py:60
  754.1 2.4 convert_add_fusion
  756.5 2.6 copy.7
  759.0 1.4 fusion.2
  761.5 11.7 %cholesky.103 = f32[128,128]{1,0:T(8,128)S(1)} custom-call(f32[128,128]{1,0:T(8,128)S(1)} %cholesky.263), custom_call_target="Cholesky" | custom-call | tf_op jit(solution)/shard_map/jit(cholesky)/cholesky | solution.py:13
  773.3 9.8 %custom-call.32 = f32[1,128,128]{1,2,0:T(8,128)S(1)} custom-call(f32[1,128,128]{2,1,0:T(8,128)S(1)} %get-tuple-element.32), custom_call_target="InvertDiagBlocksLowerTriangular" | custom-call | tf_op jit(solution)/shard_map/jit(cholesky)/cholesky | solution.py:13
  785.8 11.7 %cholesky.215 = f32[128,128]{1,0:T(8,128)S(1)} custom-call(f32[128,128]{1,0:T(8,128)S(1)} %cholesky.267), custom_call_target="Cholesky" | custom-call | tf_op jit(solution)/shard_map/jit(cholesky)/cholesky | solution.py:13
  797.8 9.9 %custom-call.33 = f32[1,128,128]{1,2,0:T(8,128)S(1)} custom-call(f32[1,128,128]{2,1,0:T(8,128)S(1)} %get-tuple-element.30), custom_call_target="InvertDiagBlocksLowerTriangular" | custom-call | tf_op jit(solution)/shard_map/jit(cholesky)/cholesky | solution.py:13
  808.1 1.5 convolution_subtract_fusion.7
  809.6 11.7 %cholesky.236 = f32[128,128]{1,0:T(8,128)S(1)} custom-call(f32[128,128]{1,0:T(8,128)S(1)} %cholesky.272), custom_call_target="Cholesky" | custom-call | tf_op jit(solution)/shard_map/jit(cholesky)/cholesky | solution.py:13
  821.5 9.8 %custom-call.34 = f32[1,128,128]{1,2,0:T(8,128)S(1)} custom-call(f32[1,128,128]{2,1,0:T(8,128)S(1)} %get-tuple-element.28), custom_call_target="InvertDiagBlocksLowerTriangular" | custom-call | tf_op jit(solution)/shard_map/jit(cholesky)/cholesky | solution.py:13
  832.9 11.9 %cholesky.253 = f32[128,128]{1,0:T(8,128)S(1)} custom-call(f32[128,128]{1,0:T(8,128)S(1)} %convolution_subtract_fusion.8), custom_call_target="Cholesky" | custom-call | tf_op jit(solution)/shard_map/jit(cholesky)/cholesky | solution.py:13
  850.6 14.2 %while.1 = (s32[]{:T(128)}, f32[512,512]{0,1:T(8,128)}, s32[4,2]{0,1:T(2,128)S(1)}, f32[4,128,128]{2,1,0:T(8,128)}, s32[]{:T(128)}) while((s32[]{:T(128)}, f32[512,512]{0,1:T(8,128)}, s32[4,2]{0,1:T(2,128)S(1)}, f32[4,128,128]{2,1,0:T(8,128)}, s32[]{:T(128)}) %tuple.27), condition=%wide.while_cond, body=%wide.while_body.sunk | while | flops 2 | bytes 393329 | solution.py:14
  851.3 2.2 dynamic-slice.7
  854.8 2.2 dynamic-slice.7
  858.4 2.2 dynamic-slice.7
  861.9 2.1 dynamic-slice.7
  864.8 40.2 %custom-call.35 = f32[4,128,128]{1,2,0:T(8,128)S(1)} custom-call(f32[4,128,128]{2,1,0:T(8,128)} %get-tuple-element.12), custom_call_target="InvertDiagBlocksLowerTriangular" | custom-call | tf_op jit(solution)/shard_map/triangular_solve | solution.py:14
  906.2 1.6 convolution_subtract_fusion.3
  908.2 1.9 convolution_subtract_fusion.2
  910.6 2.4 convolution_subtract_fusion.5
  916.6 2.4 convolution_convert_fusion
  (92 shorter events, 28.9 us)
Async XLA Ops:
  6.5 4.9 copy-start
  6.5 104.4 %reduce-scatter.2.cloned.1.call-start = ((), (), s32[]{:S(2)}) async-start(), calls=%async_computation.1 | async-start | bytes 7798784 | tf_op jit(solution)/shard_map/reduce_scatter | solution.py:42
  11.4 1.5 copy-start.6
  18.2 156.1 %all-gather.2.cloned.1.call-start = ((), (), s32[]{:S(2)}) async-start(), calls=%async_computation.2 | async-start | bytes 1949696 | tf_op jit(solution)/shard_map/all_gather | solution.py:46
  112.7 219.9 %all-reduce.5.cloned.1.call-start = ((), (), s32[]{:S(2)}) async-start(), calls=%async_computation.3 | async-start | bytes 3670016 | tf_op jit(solution)/shard_map/psum | solution.py:9
  175.7 314.2 %all-reduce.7.cloned.1.call-start = ((), (), s32[]{:S(2)}) async-start(), calls=%async_computation.4 | async-start | bytes 7340032 | tf_op jit(solution)/shard_map/psum | solution.py:53
  184.5 569.6 %all-reduce.9.cloned.1.call-start = ((), (), s32[]{:S(2)}) async-start(), calls=%async_computation.5 | async-start | bytes 2097152 | tf_op jit(solution)/shard_map/psum | solution.py:60
  489.9 2.4 copy-start.1
  492.3 2.7 copy-start.7
  494.0 1.0 copy-start.4
  754.1 4.9 copy-start.3
  760.5 1.0 copy-start.5
  864.8 43.5 %copy-start.2 = (f32[512,512]{0,1:T(8,128)S(1)}, f32[512,512]{0,1:T(8,128)}, u32[]{:S(2)}) copy-start(f32[512,512]{0,1:T(8,128)} %get-tuple-element.95) | copy-start | bytes 3145732
  914.6 2.0 copy-start.8
Sparse Core Ops, SparseCore 0:
  18.3 92.6 reduce-scatter.1
  112.9 61.4 all-gather.1
  177.0 155.6 all-reduce.4
  335.2 154.7 all-reduce.6
  495.2 258.8 all-reduce.8
where the time goes:
time: 932 us; the launch traced here: 926 us
  waiting for transfers between devices  717 us (77%)
  other arithmetic  134 us (14%)
  matrix products  34.7 us (4%)
  local copies, waits for them, and re-layouts  23.3 us (2%)
  between operations  16.3 us (2%)
    psum x1, waiting for transfers between devices, per_device(): system = identity + lax.psum(padded, ('row', 'col'))  258 us
    psum x1, waiting for transfers between devices, per_device(): image_full = lax.psum(partial_image, 'col')  157 us
    psum x1, waiting for transfers between devices, spread(): return lax.psum(jnp.where(mine, x, jnp.zeros_like(x)), axis)  148 us
    reduce_scatter x1, waiting for transfers between devices, per_device(): lax.psum_scatter(jnp.concatenate([gate_part, up_part], axis=1), 'row', sc...  92.7 us
    another operation x14, other arithmetic, right_solve(): factor = jnp.linalg.cholesky(system)  78.8 us
    all_gather x1, waiting for transfers between devices, per_device(): keys_col = lax.all_gather(keys_mine, 'row', axis=0, tiled=True)  61.5 us
    another operation x3, other arithmetic, right_solve(): lax.linalg.triangular_solve(factor, target, left_side=False, lower=True,...  41.3 us
  transfers between devices with their start and end apart: 5, of which 5 were waited for; matrix products, arithmetic and copies ran while one was open for 1% of the time, Pallas kernels for 0%

commit v1 on v0

v1 whole, which is shorter than its diff:
```python
import jax
import jax.numpy as jnp
from jax import lax
from jax.experimental import pallas as pl
from jax.experimental.pallas import tpu as pltpu
from jax.sharding import PartitionSpec as P

MESH = pl.DeviceIdType.MESH
F32 = jnp.float32
BF16 = jnp.bfloat16


def exchange_kernel(
    gu, cov_hbm, s_out, img_out,
    cov, ysend, yrecv, psend, precv, plast_s, plast_r,
    qsend, qrecv, qlast_s, qlast_r, qy_s, qy_r,
    kt, kts, cxs, cxr, cs, cr, spart, exs, exr, e1s, e1r, e2s, e2r, e3, s2,
    cov_sem, y_ss, y_rs, z_ss, z_rs, qy_ss, qy_rs, b_ss, b_rs, t_ss, t_rs,
    cx_ss, cx_rs, c_ss, c_rs, ex_ss, ex_rs, e1_ss, e1_rs, e2_ss, e2_rs,
    e3_ss, e3_rs, e4_ss, e4_rs, d_ss, d_rs, loc_sem,
):
    ch = kt.shape[0] // 16
    half = kt.shape[1] // 2
    me_r, me_c = lax.axis_index("row"), lax.axis_index("col")
    y, z = me_r // 8, me_r % 8
    g, core = me_c // 2, me_c % 2

    def send(src, dst, ss, rs, r, c):
        return pltpu.make_async_remote_copy(
            src_ref=src, dst_ref=dst, send_sem=ss, recv_sem=rs,
            device_id=(r, c), device_id_type=MESH,
        )

    def rows(i, n=ch):
        return pl.ds(pl.multiple_of(i * n, 8), n)

    y_to = ((1 - y) * 8 + z, me_c)

    def z_to(step):
        return (y * 8 + (z + step + 8) % 8, me_c)

    partner = (me_r, g * 2 + 1 - core)

    def g_to(k):
        return (me_r, ((g + k) % 8) * 2 + core)

    own_sub = core * 8 + (g + 4) % 8
    t_out = (me_c, ((me_r % 8 + 4) % 8) * 2 + me_r // 8)
    t_in = (own_sub, me_r)

    cov_copy = pltpu.make_async_copy(cov_hbm, cov, cov_sem)
    cov_copy.start()
    kts[...] = jnp.zeros_like(kts)

    barrier = pltpu.get_barrier_semaphore()
    peers = [((me_r + k) % 16, me_c) for k in range(1, 16)]
    peers += [g_to(k) for k in range(1, 8)] + [partner, t_out, t_in]
    for p in peers:
        pl.semaphore_signal(barrier, inc=1, device_id=p, device_id_type=MESH)
    pl.semaphore_wait(barrier, len(peers))

    lo, hi = pl.ds(0, half), pl.ds(half, half)
    pending = []

    ycopies = {}
    for o in (4, 3, 5, 2, 6, 1, 7, 0):
        ysend[o] = gu[:, rows((1 - y) * 8 + (z + o) % 8), lo].astype(BF16)
        ycopies[o] = send(ysend.at[o], yrecv.at[o], y_ss.at[o], y_rs.at[o], *y_to)
        ycopies[o].start()

    def p_own(o):
        return gu[:, rows(y * 8 + (z + o) % 8), lo] + yrecv[o].astype(F32)

    def q_own(o, yy):
        return gu[:, rows(yy * 8 + (z + o) % 8), hi]

    copies = {}
    for s in range(1, 5):
        for side in (0, 1):
            if side == 1 and s == 1:
                continue
            last = s == 4
            slot = side * 3 + s - 1 - side
            sign = -1 if side == 0 else 1
            o = (sign * (5 - s)) % 8
            first = s == 1 + side
            if not first:
                copies["q", side, s - 1].wait_recv()
            for yy in (0, 1):
                v = q_own(o, yy)
                if not first:
                    v = v + qrecv[slot - 1, yy].astype(F32)
                if last:
                    qlast_s[side, yy] = v
                else:
                    qsend[slot, yy] = v.astype(BF16)
            if last:
                src, dst = qlast_s.at[side], qlast_r.at[side]
            else:
                src, dst = qsend.at[slot], qrecv.at[slot]
            i = side * 4 + s - 1
            cp = send(src, dst, z_ss.at[i], z_rs.at[i], *z_to(sign))
            cp.start()
            copies["q", side, s] = cp
            sign = -sign
            o = (sign * (5 - s)) % 8
            ycopies[o].wait_recv()
            v = p_own(o)
            if not first:
                copies["p", side, s - 1].wait_recv()
                v = v + precv[slot - 1].astype(F32)
            if last:
                plast_s[side] = v
                src, dst = plast_s.at[side], plast_r.at[side]
            else:
                psend[slot] = v.astype(BF16)
                src, dst = psend.at[slot], precv.at[slot]
            i = 8 + side * 4 + s - 1
            cp = send(src, dst, z_ss.at[i], z_rs.at[i], *z_to(sign))
            cp.start()
            copies["p", side, s] = cp
    copies["q", 0, 4].wait_recv()
    copies["q", 1, 4].wait_recv()
    qy_s[...] = q_own(0, 1 - y) + qlast_r[0, 1 - y] + qlast_r[1, 1 - y]
    qy = send(qy_s, qy_r, qy_ss, qy_rs, *y_to)
    qy.start()
    ycopies[0].wait_recv()
    copies["p", 0, 4].wait_recv()
    copies["p", 1, 4].wait_recv()
    v = p_own(0) + plast_r[0] + plast_r[1]
    kt[rows(me_r), lo] = (v[0] / (1.0 + jnp.exp(-v[0])) * v[1]).astype(BF16)
    qy.wait_recv()
    v = q_own(0, y) + qlast_r[0, y] + qlast_r[1, y] + qy_r[...]
    kt[rows(me_r), hi] = (v[0] / (1.0 + jnp.exp(-v[0])) * v[1]).astype(BF16)
    pending += list(ycopies.values()) + list(copies.values()) + [qy]

    def shard(zo, rel):
        yy = y if rel == 0 else 1 - y
        return rows(yy * 8 + (zo + 8) % 8)

    mine = kt.at[rows(me_r)]
    b_y = send(mine, mine, b_ss.at[32], b_rs.at[32], *y_to)
    b_y.start()
    bc = {}

    def forward(h, side, t, rel):
        sign = 1 if h == side else -1
        ref = kt.at[shard(z - sign * (t - 1), rel), lo if h == 0 else hi]
        i = h * 16 + side * 8 + (t - 1) * 2 + rel
        cp = send(ref, ref, b_ss.at[i], b_rs.at[i], *z_to(sign))
        cp.start()
        bc[h, side, t, rel] = cp

    for side in (0, 1):
        for h in (0, 1):
            forward(h, side, 1, 0)
    tr = send(mine, kts.at[pl.ds(0, ch)], t_ss, t_rs, *t_out)
    tr.start()
    b_y.wait_recv()
    for side in (0, 1):
        for h in (0, 1):
            forward(h, side, 1, 1)
    for t in range(2, 5):
        for rel in (0, 1):
            for side in (0, 1):
                for h in (0, 1):
                    if side == 1 and t == 4:
                        continue
                    bc[h, side, t - 1, rel].wait_recv()
                    forward(h, side, t, rel)
    for rel in (0, 1):
        for h in (0, 1):
            bc[h, 1, 3, rel].wait_recv()
            bc[h, 0, 4, rel].wait_recv()
    pending += [b_y, tr] + list(bc.values())

    cov_copy.wait()

    def product(sub):
        return jnp.dot(cov[rows(sub), :], kt[...], preferred_element_type=F32)

    def sub_of(k, cc):
        return cc * 8 + (g + k + 4) % 8

    def cx_copy(k):
        return send(cxs.at[k], cxr.at[k], cx_ss.at[k], cx_rs.at[k], *partner)

    def c_copy(k):
        return send(cs.at[k], cr.at[k], c_ss.at[k], c_rs.at[k], *g_to(k))

    def far(k, carry):
        kk = (k + 1) % 8
        cxs[kk] = product(sub_of(kk, 1 - core)).astype(BF16)
        cx_copy(kk).start()
        return carry

    lax.fori_loop(0, 8, far, 0)

    def near(k, carry):
        v = product(sub_of(k, core))
        cx_copy(k).wait_recv()
        cs[k] = (v + cxr[k].astype(F32)).astype(BF16)
        c_copy(k).start()
        return carry

    lax.fori_loop(1, 8, near, 0)
    v = product(sub_of(0, core))
    cx_copy(0).wait_recv()
    v = v + cxr[0].astype(F32)
    for k in range(1, 8):
        c_copy(k).wait_recv()
        v = v + cr[k].astype(F32)
    v_hi = v.astype(BF16)
    v_lo = (v - v_hi.astype(F32)).astype(BF16)
    img_out[rows(own_sub), :] = v_hi

    tr.wait_recv()
    pad = jnp.zeros((kts.shape[0] - ch, kts.shape[1]), BF16)
    dims = (((0,), (0,)), ((), ()))
    keys_s = kts[...]
    part = lax.dot_general(
        keys_s, jnp.concatenate([v_hi, pad], 0), dims, preferred_element_type=F32
    ) + lax.dot_general(
        keys_s, jnp.concatenate([v_lo, pad], 0), dims, preferred_element_type=F32
    )
    spart[...] = part
    n2 = spart.shape[0] // 2
    exs[...] = spart[rows(1 - core, n2), :].astype(BF16)
    ex = send(exs, exr, ex_ss, ex_rs, *partner)
    ex.start()
    ex.wait_recv()
    e1s[...] = (spart[rows(core, n2), :] + exr[...].astype(F32))
    blk = n2 // 8
    e1c = []
    for k in range(1, 8):
        e2s[k] = e1s[rows((g + k) % 8, blk), :].astype(BF16)
        cp = send(e2s.at[k], e1r.at[k], e1_ss.at[k], e1_rs.at[k], *g_to(k))
        cp.start()
        e1c.append(cp)
    dc = {}
    mine = img_out.at[rows(own_sub)]

    def gather(ref_of, ss, rs, out):
        for k in range(1, 8):
            ref = ref_of(g)
            out[k] = send(ref, ref, ss.at[k], rs.at[k], *g_to(k))
            out[k].start()
        ref = ref_of(g)
        out[0] = send(ref, ref, ss.at[0], rs.at[0], *partner)
        out[0].start()

    def relay(ref_of, ss, rs, out):
        for k in range(1, 8):
            out[k].wait_recv()
            ref = ref_of((g - k + 8) % 8)
            out[7 + k] = send(ref, ref, ss.at[7 + k], rs.at[7 + k], *partner)
            out[7 + k].start()

    def img_ref(gg):
        return img_out.at[rows(core * 8 + (gg + 4) % 8)]

    def s_ref(gg):
        return s_out.at[rows(core * 8 + gg, blk)]

    gather(img_ref, d_ss, d_rs, dc)
    v = e1s[rows(g, blk), :]
    for k in range(1, 8):
        e1c[k - 1].wait_recv()
        v = v + e1r[k].astype(F32)
    s2[...] = v
    e1s[pl.ds(0, blk), :] = v
    tile = pl.ds(0, blk)

    def piece(ref, i):
        return ref.at[rows(i // 4, 8), pl.ds(pl.multiple_of(i % 4 * 128, 128), 128)]

    e2c = []
    for k in range(1, 16):
        cp = send(
            piece(e1s, (me_r + k) % 16), e2r.at[k], e2_ss.at[k], e2_rs.at[k],
            (me_r + k) % 16, me_c,
        )
        cp.start()
        e2c.append(cp)
    at_rows = rows(me_r // 4, 8)
    at_cols = pl.ds(pl.multiple_of(me_r % 4 * 128, 128), 128)
    v = e1s[at_rows, at_cols]
    for k in range(1, 16):
        e2c[k - 1].wait_recv()
        v = v + e2r[k]
    e3[...] = v
    e3c = []
    for k in range(1, 16):
        cp = send(
            e3, s2.at[at_rows, at_cols], e3_ss.at[k], e3_rs.at[k],
            (me_r + k) % 16, me_c,
        )
        cp.start()
        e3c.append(cp)
    s2[at_rows, at_cols] = v
    for cp in e3c:
        cp.wait_recv()
    s_out[rows(core * 8 + g, blk), :] = s2[...]
    ec = {}
    gather(s_ref, e4_ss, e4_rs, ec)
    relay(s_ref, e4_ss, e4_rs, ec)
    relay(img_ref, d_ss, d_rs, dc)
    for out in (ec, dc):
        out[0].wait_recv()
        for k in range(1, 8):
            out[7 + k].wait_recv()
    pending += [ex] + e1c + e2c + e3c + list(ec.values()) + list(dc.values())
    for cp in pending:
        cp.wait_send()
    for k in range(8):
        cx_copy(k).wait_send()
    for k in range(1, 8):
        c_copy(k).wait_send()


def exchange(gu, inv_cov):
    ff, facts = gu.shape[1:]
    ch, half, blk = ff // 16, facts // 2, facts // 16
    dma = pltpu.SemaphoreType.DMA
    vm = pltpu.VMEM
    scratch = [
        vm(inv_cov.shape, BF16),
        vm((8, 2, ch, half), BF16), vm((8, 2, ch, half), BF16),
        vm((5, 2, ch, half), BF16), vm((5, 2, ch, half), BF16),
        vm((2, 2, ch, half), F32), vm((2, 2, ch, half), F32),
        vm((5, 2, 2, ch, half), BF16), vm((5, 2, 2, ch, half), BF16),
        vm((2, 2, 2, ch, half), F32), vm((2, 2, 2, ch, half), F32),
        vm((2, ch, half), F32), vm((2, ch, half), F32),
        vm((ff, facts), BF16), vm((-(-ch // 128) * 128, facts), BF16),
        vm((8, ch, facts), BF16), vm((8, ch, facts), BF16),
        vm((8, ch, facts), BF16), vm((8, ch, facts), BF16),
        vm((facts, facts), F32),
        vm((facts // 2, facts), BF16), vm((facts // 2, facts), BF16),
        vm((facts // 2, facts), F32), vm((8, blk, facts), BF16),
        vm((8, blk, facts), BF16), vm((16, 8, 128), F32), vm((8, 128), F32),
        vm((blk, facts), F32),
        dma(()), dma((8,)), dma((8,)), dma((16,)), dma((16,)), dma(()), dma(()),
        dma((33,)), dma((33,)), dma(()), dma(()),
        dma((8,)), dma((8,)), dma((8,)), dma((8,)), dma(()), dma(()),
        dma((8,)), dma((8,)), dma((16,)), dma((16,)), dma((16,)), dma((16,)),
        dma((15,)), dma((15,)), dma((15,)), dma((15,)), dma(()),
    ]
    return pl.pallas_call(
        exchange_kernel,
        name="exchange",
        out_shape=(
            jax.ShapeDtypeStruct((facts, facts), F32),
            jax.ShapeDtypeStruct((ff, facts), BF16),
        ),
        in_specs=[
            pl.BlockSpec(memory_space=pltpu.VMEM),
            pl.BlockSpec(memory_space=pl.ANY),
        ],
        out_specs=[pl.BlockSpec(memory_space=pltpu.VMEM)] * 2,
        scratch_shapes=scratch,
        compiler_params=pltpu.CompilerParams(
            collective_id=0, has_side_effects=True, vmem_limit_bytes=60 * 2**20
        ),
    )(gu, inv_cov)


def right_solve(system, target):
    factor = jnp.linalg.cholesky(system)
    halfway = lax.linalg.triangular_solve(
        factor, target, left_side=False, lower=True, transpose_a=True
    )
    return lax.linalg.triangular_solve(
        factor, halfway, left_side=False, lower=True, transpose_a=False
    )


def per_device(hidden, positions, gate_weight, up_weight, inv_cov, target_res):
    facts = positions.shape[0]
    subject = jnp.take(hidden, positions, axis=0)
    dims = (((0,), (1,)), ((), ()))
    gate = lax.dot_general(gate_weight, subject, dims, preferred_element_type=F32)
    up = lax.dot_general(up_weight, subject, dims, preferred_element_type=F32)
    system, image_t = exchange(jnp.stack([gate, up]), inv_cov)
    system = system + jnp.eye(facts, dtype=F32)
    coeffs = right_solve(system, target_res.astype(F32)).astype(BF16)
    return lax.dot_general(
        coeffs, image_t, (((1,), (1,)), ((), ())), preferred_element_type=F32
    ).astype(BF16)


def solution(mesh):
    return jax.shard_map(
        per_device,
        mesh=mesh,
        in_specs=(
            P(None, "row"),
            P(),
            P("row", "col"),
            P("row", "col"),
            P("row", "col"),
            P("col", None),
        ),
        out_specs=P("col", "row"),
        check_vma=False,
    )
```

time: 932 us -> 315 us (0.34)
  waiting for transfers between devices: 717 us -> 0 us
  Pallas kernels: 0 us -> 139 us
  matrix products: 34.7 us -> 18.9 us
  between operations: 16.3 us -> 3.14 us
    psum x3 -> x0, waiting for transfers between devices: 563 us -> none  [the longest x1 258 us: per_device(): system = identity + lax.psum(padded, ('row', 'col'))]
    pallas_call x0 -> x1, Pallas kernels: none -> 139 us  [exchange(): pl.pallas_call(exchange_kernel, name='exchange', out_shape=(jax.ShapeDtyp...]
    reduce_scatter x1 -> x0, waiting for transfers between devices: 92.7 us -> none  [per_device(): lax.psum_scatter(jnp.concatenate([gate_part, up_part], axis=1), 'row', sc...]
    all_gather x1 -> x0, waiting for transfers between devices: 61.5 us -> none  [per_device(): keys_col = lax.all_gather(keys_mine, 'row', axis=0, tiled=True)]
    dot_general x6 -> x3, matrix products: 17.3 us -> 4.88 us  [the longest x1 2.4 us: per_device(): lax.dot_general(coeffs, image_t, (((1,), (1,)), ((), ())), preferred_elem...]
  transfers between devices with their start and end apart: 5 -> 0, of which waited for: 5 -> 0; matrix products, arithmetic and copies ran while one was open for 1% -> 0% of each run, Pallas kernels for 0% -> 0%
where the time goes in v1:
time: 315 us; the launch traced here: 310 us
  Pallas kernels  139 us (44%)
  other arithmetic  128 us (41%)
  local copies, waits for them, and re-layouts  20.5 us (7%)
  matrix products  18.9 us (6%)
    pallas_call x1, Pallas kernels, exchange(): pl.pallas_call(exchange_kernel, name='exchange', out_shape=(jax.ShapeDtyp...  139 us
    another operation x14, other arithmetic, right_solve(): factor = jnp.linalg.cholesky(system)  79 us
    another operation x3, other arithmetic, right_solve(): lax.linalg.triangular_solve(factor, target, left_side=False, lower=True,...  40.4 us
    another operation x12, local copies, waits for them, and re-layouts  11.6 us

profile of v1, /device:TPU:1, one launch (start us, length us, event | category | flops | bytes accessed | tf_op | source)
XLA Modules:
  0.0 309.8 jit_solution(4680658215382317444)
XLA Ops:
  0.8 3.4 %gather_fusion = bf16[512,512]{1,0:T(8,128)(2,1)S(1)} fusion(bf16[1024,512]{1,0:T(8,128)(2,1)} %param.6, s32[1024]{0:T(1024)S(1)} %pad_clamp_fusion), kind=kCustom, calls=%fused_computation | custom fusion | bytes 1050624 | tf_op jit(solution)/shard_map/jit(_take)/gather | solution.py:379
  4.2 1.2 convolution_bitcast_fusion
  5.7 1.2 convolution_bitcast_fusion.1
  7.0 3.8 %pad_maximum_fusion.gu = f32[2,1792,512]{2,1,0:T(8,128)} fusion(f32[1,1792,512]{2,1,0:T(8,128)S(1)} %convolution_bitcast_fusion, f32[1,1792,512]{2,1,0:T(8,128)S(1)} %convolution_bitcast_fusion.1), kind=kLoop, calls=%fused_computation.3 | loop fusion | flops 1835008 | bytes 14680064 | tf_op jit(solution)/shard_map/stack | solution.py:383
  10.8 139.4 %exchange.1 = (f32[512,512]{1,0:T(8,128)}, bf16[1792,512]{1,0:T(8,128)(2,1)}) custom-call(f32[2,1792,512]{2,1,0:T(8,128)} %pad_maximum_fusion.gu, bf16[1792,1792]{1,0:T(8,128)(2,1)} %cov_hbm.1), custom_call_target="tpu_custom_call" | custom-call | tf_op jit(solution)/shard_map/exchange/pallas_call | solution.py:348
  150.2 1.6 copy.9
  151.8 1.1 convert_add_fusion
  152.9 2.5 copy.10
  155.4 1.4 fusion
  157.9 11.7 %cholesky.104 = f32[128,128]{1,0:T(8,128)S(1)} custom-call(f32[128,128]{1,0:T(8,128)S(1)} %cholesky.266), custom_call_target="Cholesky" | custom-call | tf_op jit(solution)/shard_map/jit(cholesky)/cholesky | solution.py:368
  169.6 9.8 %custom-call.32 = f32[1,128,128]{1,2,0:T(8,128)S(1)} custom-call(f32[1,128,128]{2,1,0:T(8,128)S(1)} %get-tuple-element.36), custom_call_target="InvertDiagBlocksLowerTriangular" | custom-call | tf_op jit(solution)/shard_map/jit(cholesky)/cholesky | solution.py:368
  179.5 1.2 constant_dynamic-update-slice_fusion.3
  180.8 1.3 convolution_subtract_fusion.6
  182.1 12.1 %cholesky.217 = f32[128,128]{1,0:T(8,128)S(1)} custom-call(f32[128,128]{1,0:T(8,128)S(1)} %cholesky.270), custom_call_target="Cholesky" | custom-call | tf_op jit(solution)/shard_map/jit(cholesky)/cholesky | solution.py:368
  196.2 9.8 %custom-call.33 = f32[1,128,128]{1,2,0:T(8,128)S(1)} custom-call(f32[1,128,128]{2,1,0:T(8,128)S(1)} %get-tuple-element.33), custom_call_target="InvertDiagBlocksLowerTriangular" | custom-call | tf_op jit(solution)/shard_map/jit(cholesky)/cholesky | solution.py:368
  206.3 1.3 convolution_subtract_fusion.7
  207.6 11.7 %cholesky.238 = f32[128,128]{1,0:T(8,128)S(1)} custom-call(f32[128,128]{1,0:T(8,128)S(1)} %cholesky.275), custom_call_target="Cholesky" | custom-call | tf_op jit(solution)/shard_map/jit(cholesky)/cholesky | solution.py:368
  220.7 9.8 %custom-call.34 = f32[1,128,128]{1,2,0:T(8,128)S(1)} custom-call(f32[1,128,128]{2,1,0:T(8,128)S(1)} %get-tuple-element.30), custom_call_target="InvertDiagBlocksLowerTriangular" | custom-call | tf_op jit(solution)/shard_map/jit(cholesky)/cholesky | solution.py:368
  230.8 1.2 convolution_subtract_fusion.8
  232.0 11.9 %cholesky.255 = f32[128,128]{1,0:T(8,128)S(1)} custom-call(f32[128,128]{1,0:T(8,128)S(1)} %convolution_subtract_fusion.8), custom_call_target="Cholesky" | custom-call | tf_op jit(solution)/shard_map/jit(cholesky)/cholesky | solution.py:368
  245.2 1.1 select_select_fusion
  246.3 11.7 %while.1 = (s32[]{:T(128)}, f32[512,512]{1,0:T(8,128)}, s32[4,2]{0,1:T(2,128)S(1)}, f32[4,128,128]{2,1,0:T(8,128)S(1)}, s32[]{:T(128)}) while((s32[]{:T(128)}, f32[512,512]{1,0:T(8,128)}, s32[4,2]{0,1:T(2,128)S(1)}, f32[4,128,128]{2,1,0:T(8,128)S(1)}, s32[]{:T(128)}) %tuple.30), condition=%wide.while_cond, body=%wide.while_body.sunk | while | flops 2 | bytes 131181 | solution.py:369
  247.0 2.2 bitcast_dynamic-update-slice_fusion.2
  249.9 2.2 bitcast_dynamic-update-slice_fusion.2
  252.9 2.2 bitcast_dynamic-update-slice_fusion.2
  255.8 2.2 bitcast_dynamic-update-slice_fusion.2
  258.0 39.3 %custom-call.35 = f32[4,128,128]{1,2,0:T(8,128)S(1)} custom-call(f32[4,128,128]{2,1,0:T(8,128)S(1)} %get-tuple-element.16), custom_call_target="InvertDiagBlocksLowerTriangular" | custom-call | tf_op jit(solution)/shard_map/triangular_solve | solution.py:369
  297.3 1.2 fusion.34
  298.6 1.2 convert_element_type.11
  300.8 1.0 convolution_subtract_fusion.2
  302.2 1.5 convolution_subtract_fusion.5
  307.2 2.4 convolution_convert_fusion
  (50 shorter events, 12.5 us)
Async XLA Ops:
  0.0 4.2 %copy-start = (bf16[512,1792]{1,0:T(8,128)(2,1)S(1)}, bf16[512,1792]{1,0:T(8,128)(2,1)}, u32[]{:S(2)}) copy-start(bf16[512,1792]{1,0:T(8,128)(2,1)} %param.9) | copy-start | bytes 5505028
  0.8 3.4 %copy-start.4 = (s32[512]{0:T(512)S(1)}, s32[512]{0:T(512)}, u32[]{:S(2)}) copy-start(s32[512]{0:T(512)} %param.7) | copy-start | bytes 6148
  4.2 1.5 copy-start.3
  156.9 1.0 copy-start.2
  258.0 41.7 %copy-start.1 = (f32[512,512]{1,0:T(8,128)S(1)}, f32[512,512]{1,0:T(8,128)}, u32[]{:S(2)}) copy-start(f32[512,512]{1,0:T(8,128)} %get-tuple-element.91) | copy-start | bytes 3145732
  305.2 2.0 copy-start.5

commit v2 on v1

--- a/solution.py
+++ b/solution.py
@@ -364,28 +364,77 @@
     )(gu, inv_cov)
 
 
-def right_solve(system, target):
-    factor = jnp.linalg.cholesky(system)
-    halfway = lax.linalg.triangular_solve(
-        factor, target, left_side=False, lower=True, transpose_a=True
+def invert(m):
+    n = m.shape[0]
+    lane = lax.broadcasted_iota(jnp.int32, (1, n), 1)
+    sub = lax.broadcasted_iota(jnp.int32, (n, 1), 0)
+    for p in range(n):
+        row = m[p : p + 1, :]
+        col = m[:, p : p + 1]
+        r = 1.0 / jnp.broadcast_to(m[p : p + 1, p : p + 1], (1, n))
+        row = jnp.where(lane == p, r, row * r)
+        m = jnp.where(sub == p, row, jnp.where(lane == p, 0.0, m) - col * row)
+    return m
+
+
+def solve_kernel(s_ref, t_ref, img_ref, out_ref, a):
+    n = s_ref.shape[0]
+    b = min(128, n)
+    eye = lax.broadcasted_iota(jnp.int32, (n, n), 0) == lax.broadcasted_iota(
+        jnp.int32, (n, n), 1
     )
-    return lax.linalg.triangular_solve(
-        factor, halfway, left_side=False, lower=True, transpose_a=False
-    )
+    a[...] = s_ref[...] + jnp.where(eye, 1.0, 0.0)
+
+    def dot(p, q):
+        return jnp.dot(p, q, precision=lax.Precision.HIGHEST, preferred_element_type=F32)
+
+    def block(k, carry):
+        d = pl.ds(pl.multiple_of(k * b, b), b)
+        inv = invert(a[d, d])
+        col = a[:, d]
+        wide = dot(inv, a[d, :])
+        a[...] = a[...] - dot(col, wide)
+        a[:, d] = -dot(col, inv)
+        a[d, :] = wide
+        a[d, d] = inv
+        return carry
+
+    lax.fori_loop(0, n // b, block, 0)
+    v = a[...]
+    coeffs = jnp.zeros((t_ref.shape[0], n), F32)
+    for _ in range(3):
+        short = v.astype(BF16)
+        coeffs = coeffs + jnp.dot(t_ref[...], short, preferred_element_type=F32)
+        v = v - short.astype(F32)
+    coeffs = coeffs.astype(BF16)
+    w = 256
+    for j in range(out_ref.shape[1] // w):
+        out_ref[:, j * w : (j + 1) * w] = lax.dot_general(
+            coeffs, img_ref[j * w : (j + 1) * w, :], (((1,), (1,)), ((), ())),
+            preferred_element_type=F32,
+        ).astype(BF16)
+
+
+def solve(system, target, image_t):
+    n = system.shape[0]
+    return pl.pallas_call(
+        solve_kernel,
+        name="solve",
+        out_shape=jax.ShapeDtypeStruct((target.shape[0], image_t.shape[0]), BF16),
+        in_specs=[pl.BlockSpec(memory_space=pltpu.VMEM)] * 3,
+        out_specs=pl.BlockSpec(memory_space=pltpu.VMEM),
+        scratch_shapes=[pltpu.VMEM((n, n), F32)],
+        compiler_params=pltpu.CompilerParams(vmem_limit_bytes=40 * 2**20),
+    )(system, target, image_t)
 
 
 def per_device(hidden, positions, gate_weight, up_weight, inv_cov, target_res):
-    facts = positions.shape[0]
     subject = jnp.take(hidden, positions, axis=0)
     dims = (((0,), (1,)), ((), ()))
     gate = lax.dot_general(gate_weight, subject, dims, preferred_element_type=F32)
     up = lax.dot_general(up_weight, subject, dims, preferred_element_type=F32)
     system, image_t = exchange(jnp.stack([gate, up]), inv_cov)
-    system = system + jnp.eye(facts, dtype=F32)
-    coeffs = right_solve(system, target_res.astype(F32)).astype(BF16)
-    return lax.dot_general(
-        coeffs, image_t, (((1,), (1,)), ((), ())), preferred_element_type=F32
-    ).astype(BF16)
+    return solve(system, target_res, image_t)
 
 
 def solution(mesh):

time: 315 us -> 208 us (0.66); the launches traced: 310 us -> 207 us
  other arithmetic: 128 us -> 5.3 us
  Pallas kernels: 139 us -> 193 us
  matrix products: 18.9 us -> 2.47 us
  local copies, waits for them, and re-layouts: 20.5 us -> 6.31 us
    another operation x17 -> x0, other arithmetic: 119 us -> none  [the longest x14 79 us: right_solve(): factor = jnp.linalg.cholesky(system)]
    pallas_call x0 -> x1, Pallas kernels: none -> 53.8 us  [solve(): pl.pallas_call(solve_kernel, name='solve', out_shape=jax.ShapeDtypeStruct...]
    another operation x20 -> x0, matrix products: 14.1 us -> none  [the longest x6 5.46 us: right_solve(): factor = jnp.linalg.cholesky(system)]
    another operation x17 -> x0, local copies, waits for them, and re-layouts: 11.8 us -> none
where the time goes in v2:
time: 208 us; the launch traced here: 207 us
  Pallas kernels  193 us (93%)
  local copies, waits for them, and re-layouts  6.31 us (3%)
  other arithmetic  5.3 us (3%)
  matrix products  2.47 us (1%)
    pallas_call x1, Pallas kernels, exchange(): pl.pallas_call(exchange_kernel, name='exchange', out_shape=(jax.ShapeDtyp...  139 us
    pallas_call x1, Pallas kernels, solve(): pl.pallas_call(solve_kernel, name='solve', out_shape=jax.ShapeDtypeStruct...  53.8 us

profile of v2, /device:TPU:1, one launch (start us, length us, event | category | flops | bytes accessed | tf_op | source)
XLA Modules:
  0.0 207.4 jit_solution(154642138443809538)
XLA Ops:
  0.0 0.0 copy-start
  0.0 0.8 compare_and_fusion
  0.8 0.7 compare_select_fusion
  1.5 3.3 %gather_fusion = bf16[512,512]{1,0:T(8,128)(2,1)S(1)} fusion(bf16[1024,512]{1,0:T(8,128)(2,1)} %param.6, s32[1024]{0:T(1024)S(1)} %pad_clamp_fusion), kind=kCustom, calls=%fused_computation | custom fusion | bytes 1050624 | tf_op jit(solution)/shard_map/jit(_take)/gather | solution.py:432
  4.9 0.0 copy-done
  4.9 0.0 copy-start.4
  4.9 1.2 convolution_bitcast_fusion
  6.1 0.2 copy-done.4
  6.4 1.2 convolution_bitcast_fusion.1
  7.6 3.8 %pad_maximum_fusion.gu = f32[2,1792,512]{2,1,0:T(8,128)} fusion(f32[1,1792,512]{2,1,0:T(8,128)S(1)} %convolution_bitcast_fusion, f32[1,1792,512]{2,1,0:T(8,128)S(1)} %convolution_bitcast_fusion.1), kind=kLoop, calls=%fused_computation.1 | loop fusion | flops 1835008 | bytes 14680064 | tf_op jit(solution)/shard_map/stack | solution.py:436
  11.4 0.0 copy-start.3
  11.4 139.4 %exchange.1 = (f32[512,512]{1,0:T(8,128)}, bf16[1792,512]{1,0:T(8,128)(2,1)}) custom-call(f32[2,1792,512]{2,1,0:T(8,128)} %pad_maximum_fusion.gu, bf16[1792,1792]{1,0:T(8,128)(2,1)} %cov_hbm.1), custom_call_target="tpu_custom_call" | custom-call | tf_op jit(solution)/shard_map/exchange/pallas_call | solution.py:348
  150.8 0.0 copy-done.3
  150.8 0.0 copy-start.1
  150.8 1.5 copy-done.1
  152.3 0.0 copy-start.2
  152.3 1.2 copy-done.2
  153.6 53.8 %solve.1 = bf16[512,1792]{1,0:T(8,128)(2,1)} custom-call(f32[512,512]{1,0:T(8,128)S(1)} %copy-done.2, bf16[512,512]{1,0:T(8,128)(2,1)S(1)} %copy-done.3, bf16[1792,512]{1,0:T(8,128)(2,1)S(1)} %copy-done.1), custom_call_target="tpu_custom_call" | custom-call | tf_op jit(solution)/shard_map/solve/pallas_call | solution.py:420
  (1 shorter events, 0.0 us)
Async XLA Ops:
  0.0 4.9 %copy-start = (bf16[512,1792]{1,0:T(8,128)(2,1)S(1)}, bf16[512,1792]{1,0:T(8,128)(2,1)}, u32[]{:S(2)}) copy-start(bf16[512,1792]{1,0:T(8,128)(2,1)} %param.9) | copy-start | bytes 5505028
  4.9 1.5 copy-start.4
  11.4 139.4 %copy-start.3 = (bf16[512,512]{1,0:T(8,128)(2,1)S(1)}, bf16[512,512]{1,0:T(8,128)(2,1)}, u32[]{:S(2)}) copy-start(bf16[512,512]{1,0:T(8,128)(2,1)} %t_ref.1) | copy-start | bytes 1572868
  150.8 1.5 copy-start.1
  152.3 1.2 copy-start.2

commit v3 on v2

--- a/solution.py
+++ b/solution.py
@@ -11,9 +11,8 @@
 
 
 def exchange_kernel(
-    gu, cov_hbm, s_out, img_out,
-    cov, ysend, yrecv, psend, precv, plast_s, plast_r,
-    qsend, qrecv, qlast_s, qlast_r, qy_s, qy_r,
+    gate, up, cov_hbm, s_out, img_out,
+    cov, ysend, yrecv, psend, precv, qsend, qrecv, qy_s, qy_r,
     kt, kts, cxs, cxr, cs, cr, spart, exs, exr, e1s, e1r, e2s, e2r, e3, s2,
     cov_sem, y_ss, y_rs, z_ss, z_rs, qy_ss, qy_rs, b_ss, b_rs, t_ss, t_rs,
     cx_ss, cx_rs, c_ss, c_rs, ex_ss, ex_rs, e1_ss, e1_rs, e2_ss, e2_rs,
@@ -57,80 +56,69 @@
     peers += [g_to(k) for k in range(1, 8)] + [partner, t_out, t_in]
     for p in peers:
         pl.semaphore_signal(barrier, inc=1, device_id=p, device_id_type=MESH)
-    pl.semaphore_wait(barrier, len(peers))
-
     lo, hi = pl.ds(0, half), pl.ds(half, half)
     pending = []
 
+    def projections(r, lanes):
+        return jnp.stack([gate[rows(r), lanes], up[rows(r), lanes]])
+
+    order = (4, 3, 5, 2, 6, 1, 7, 0)
+    for o in order:
+        ysend[o] = projections((1 - y) * 8 + (z + o) % 8, lo).astype(BF16)
+    pl.semaphore_wait(barrier, len(peers))
     ycopies = {}
-    for o in (4, 3, 5, 2, 6, 1, 7, 0):
-        ysend[o] = gu[:, rows((1 - y) * 8 + (z + o) % 8), lo].astype(BF16)
+    for o in order:
         ycopies[o] = send(ysend.at[o], yrecv.at[o], y_ss.at[o], y_rs.at[o], *y_to)
         ycopies[o].start()
 
     def p_own(o):
-        return gu[:, rows(y * 8 + (z + o) % 8), lo] + yrecv[o].astype(F32)
+        return projections(y * 8 + (z + o) % 8, lo) + yrecv[o].astype(F32)
 
     def q_own(o, yy):
-        return gu[:, rows(yy * 8 + (z + o) % 8), hi]
+        return projections(yy * 8 + (z + o) % 8, hi)
 
     copies = {}
     for s in range(1, 5):
-        for side in (0, 1):
-            if side == 1 and s == 1:
-                continue
-            last = s == 4
-            slot = side * 3 + s - 1 - side
-            sign = -1 if side == 0 else 1
-            o = (sign * (5 - s)) % 8
-            first = s == 1 + side
-            if not first:
-                copies["q", side, s - 1].wait_recv()
-            for yy in (0, 1):
-                v = q_own(o, yy)
-                if not first:
-                    v = v + qrecv[slot - 1, yy].astype(F32)
-                if last:
-                    qlast_s[side, yy] = v
+        for chain in range(3):
+            for side in (0, 1):
+                if side == 1 and s == 1:
+                    continue
+                slot = side * 4 + s - 1 - side
+                sign = (-1 if side == 0 else 1) * (-1 if chain == 2 else 1)
+                o = (sign * (5 - s)) % 8
+                if chain == 2:
+                    ycopies[o].wait_recv()
+                    v = p_own(o)
+                    src, dst = psend.at[slot], precv
                 else:
-                    qsend[slot, yy] = v.astype(BF16)
-            if last:
-                src, dst = qlast_s.at[side], qlast_r.at[side]
-            else:
-                src, dst = qsend.at[slot], qrecv.at[slot]
-            i = side * 4 + s - 1
-            cp = send(src, dst, z_ss.at[i], z_rs.at[i], *z_to(sign))
-            cp.start()
-            copies["q", side, s] = cp
-            sign = -sign
-            o = (sign * (5 - s)) % 8
-            ycopies[o].wait_recv()
-            v = p_own(o)
-            if not first:
-                copies["p", side, s - 1].wait_recv()
-                v = v + precv[slot - 1].astype(F32)
-            if last:
-                plast_s[side] = v
-                src, dst = plast_s.at[side], plast_r.at[side]
-            else:
-                psend[slot] = v.astype(BF16)
-                src, dst = psend.at[slot], precv.at[slot]
-            i = 8 + side * 4 + s - 1
-            cp = send(src, dst, z_ss.at[i], z_rs.at[i], *z_to(sign))
-            cp.start()
-            copies["p", side, s] = cp
-    copies["q", 0, 4].wait_recv()
-    copies["q", 1, 4].wait_recv()
-    qy_s[...] = q_own(0, 1 - y) + qlast_r[0, 1 - y] + qlast_r[1, 1 - y]
+                    v = q_own(o, chain)
+                    src, dst = qsend.at[slot, chain], qrecv.at[:, chain]
+                if s > 1 + side:
+                    copies[chain, side, s - 1].wait_recv()
+                    v = v + dst[slot - 1].astype(F32)
+                src[...] = v.astype(BF16)
+                i = chain * 8 + side * 4 + s - 1
+                cp = send(src, dst.at[slot], z_ss.at[i], z_rs.at[i], *z_to(sign))
+                cp.start()
+                copies[chain, side, s] = cp
+    for chain in (0, 1):
+        copies[chain, 0, 4].wait_recv()
+        copies[chain, 1, 4].wait_recv()
+
+    def q_sum(yy):
+        return q_own(0, yy) + qrecv[3, yy].astype(F32) + qrecv[6, yy].astype(F32)
+
+    qy_s[...] = q_sum(1 - y)
     qy = send(qy_s, qy_r, qy_ss, qy_rs, *y_to)
     qy.start()
     ycopies[0].wait_recv()
-    copies["p", 0, 4].wait_recv()
-    copies["p", 1, 4].wait_recv()
-    v = p_own(0) + plast_r[0] + plast_r[1]
+    copies[2, 0, 4].wait_recv()
+    copies[2, 1, 4].wait_recv()
+    v = p_own(0) + precv[3].astype(F32) + precv[6].astype(F32)
     kt[rows(me_r), lo] = (v[0] / (1.0 + jnp.exp(-v[0])) * v[1]).astype(BF16)
+    v = q_sum(y)
     qy.wait_recv()
-    v = q_own(0, y) + qlast_r[0, y] + qlast_r[1, y] + qy_r[...]
+    v = v + qy_r[...]
     kt[rows(me_r), hi] = (v[0] / (1.0 + jnp.exp(-v[0])) * v[1]).astype(BF16)
     pending += list(ycopies.values()) + list(copies.values()) + [qy]
 
@@ -139,40 +127,45 @@
         return rows(yy * 8 + (zo + 8) % 8)
 
     mine = kt.at[rows(me_r)]
-    b_y = send(mine, mine, b_ss.at[32], b_rs.at[32], *y_to)
-    b_y.start()
     bc = {}
+
+    def share(ref, i, to, key):
+        bc[key] = send(ref, ref, b_ss.at[i], b_rs.at[i], *to)
+        bc[key].start()
 
     def forward(h, side, t, rel):
         sign = 1 if h == side else -1
         ref = kt.at[shard(z - sign * (t - 1), rel), lo if h == 0 else hi]
-        i = h * 16 + side * 8 + (t - 1) * 2 + rel
-        cp = send(ref, ref, b_ss.at[i], b_rs.at[i], *z_to(sign))
-        cp.start()
-        bc[h, side, t, rel] = cp
-
+        share(ref, h * 16 + side * 8 + (t - 1) * 2 + rel, z_to(sign), (h, side, t, rel))
+
+    def across(side, t):
+        zo = z + (t if side == 0 else -t)
+        share(kt.at[shard(zo, 0), hi], 33 + side * 4 + t, y_to, ("y", side, t))
+
+    share(kt.at[rows(me_r), lo], 32, y_to, "y")
     for side in (0, 1):
-        for h in (0, 1):
-            forward(h, side, 1, 0)
+        forward(0, side, 1, 0)
+        forward(1, side, 1, 0)
+    across(0, 0)
     tr = send(mine, kts.at[pl.ds(0, ch)], t_ss, t_rs, *t_out)
     tr.start()
-    b_y.wait_recv()
+    bc["y"].wait_recv()
     for side in (0, 1):
-        for h in (0, 1):
-            forward(h, side, 1, 1)
-    for t in range(2, 5):
-        for rel in (0, 1):
+        forward(0, side, 1, 1)
+    for t in range(2, 6):
+        for h, rel in ((0, 0), (1, 0), (0, 1)):
             for side in (0, 1):
-                for h in (0, 1):
-                    if side == 1 and t == 4:
-                        continue
-                    bc[h, side, t - 1, rel].wait_recv()
+                if t - 1 > 4 - side:
+                    continue
+                bc[h, side, t - 1, rel].wait_recv()
+                if t <= 4 - side:
                     forward(h, side, t, rel)
-    for rel in (0, 1):
-        for h in (0, 1):
-            bc[h, 1, 3, rel].wait_recv()
-            bc[h, 0, 4, rel].wait_recv()
-    pending += [b_y, tr] + list(bc.values())
+                if h == 1:
+                    across(side, t - 1)
+    for key in list(bc):
+        if key != "y" and key[0] == "y":
+            bc[key].wait_recv()
+    pending += [tr] + list(bc.values())
 
     cov_copy.wait()
 
@@ -188,22 +181,25 @@
     def c_copy(k):
         return send(cs.at[k], cr.at[k], c_ss.at[k], c_rs.at[k], *g_to(k))
 
-    def far(k, carry):
-        kk = (k + 1) % 8
-        cxs[kk] = product(sub_of(kk, 1 - core)).astype(BF16)
-        cx_copy(kk).start()
-        return carry
-
-    lax.fori_loop(0, 8, far, 0)
-
-    def near(k, carry):
+    def far(k):
+        cxs[k] = product(sub_of(k, 1 - core)).astype(BF16)
+        cx_copy(k).start()
+
+    def near(k):
         v = product(sub_of(k, core))
         cx_copy(k).wait_recv()
         cs[k] = (v + cxr[k].astype(F32)).astype(BF16)
         c_copy(k).start()
+
+    def step(k, carry):
+        far((k + 3) % 8)
+        near(k + 1)
         return carry
 
-    lax.fori_loop(1, 8, near, 0)
+    far(1)
+    far(2)
+    lax.fori_loop(0, 6, step, 0)
+    near(7)
     v = product(sub_of(0, core))
     cx_copy(0).wait_recv()
     v = v + cxr[0].astype(F32)
@@ -318,18 +314,16 @@
         c_copy(k).wait_send()
 
 
-def exchange(gu, inv_cov):
-    ff, facts = gu.shape[1:]
+def exchange(gate, up, inv_cov):
+    ff, facts = gate.shape
     ch, half, blk = ff // 16, facts // 2, facts // 16
     dma = pltpu.SemaphoreType.DMA
     vm = pltpu.VMEM
     scratch = [
         vm(inv_cov.shape, BF16),
         vm((8, 2, ch, half), BF16), vm((8, 2, ch, half), BF16),
-        vm((5, 2, ch, half), BF16), vm((5, 2, ch, half), BF16),
-        vm((2, 2, ch, half), F32), vm((2, 2, ch, half), F32),
-        vm((5, 2, 2, ch, half), BF16), vm((5, 2, 2, ch, half), BF16),
-        vm((2, 2, 2, ch, half), F32), vm((2, 2, 2, ch, half), F32),
+        vm((7, 2, ch, half), BF16), vm((7, 2, ch, half), BF16),
+        vm((7, 2, 2, ch, half), BF16), vm((7, 2, 2, ch, half), BF16),
         vm((2, ch, half), F32), vm((2, ch, half), F32),
         vm((ff, facts), BF16), vm((-(-ch // 128) * 128, facts), BF16),
         vm((8, ch, facts), BF16), vm((8, ch, facts), BF16),
@@ -339,8 +333,8 @@
         vm((facts // 2, facts), F32), vm((8, blk, facts), BF16),
         vm((8, blk, facts), BF16), vm((16, 8, 128), F32), vm((8, 128), F32),
         vm((blk, facts), F32),
-        dma(()), dma((8,)), dma((8,)), dma((16,)), dma((16,)), dma(()), dma(()),
-        dma((33,)), dma((33,)), dma(()), dma(()),
+        dma(()), dma((8,)), dma((8,)), dma((24,)), dma((24,)), dma(()), dma(()),
+        dma((41,)), dma((41,)), dma(()), dma(()),
         dma((8,)), dma((8,)), dma((8,)), dma((8,)), dma(()), dma(()),
         dma((8,)), dma((8,)), dma((16,)), dma((16,)), dma((16,)), dma((16,)),
         dma((15,)), dma((15,)), dma((15,)), dma((15,)), dma(()),
@@ -354,6 +348,7 @@
         ),
         in_specs=[
             pl.BlockSpec(memory_space=pltpu.VMEM),
+            pl.BlockSpec(memory_space=pltpu.VMEM),
             pl.BlockSpec(memory_space=pl.ANY),
         ],
         out_specs=[pl.BlockSpec(memory_space=pltpu.VMEM)] * 2,
@@ -361,19 +356,29 @@
         compiler_params=pltpu.CompilerParams(
             collective_id=0, has_side_effects=True, vmem_limit_bytes=60 * 2**20
         ),
-    )(gu, inv_cov)
+    )(gate, up, inv_cov)
 
 
 def invert(m):
     n = m.shape[0]
     lane = lax.broadcasted_iota(jnp.int32, (1, n), 1)
     sub = lax.broadcasted_iota(jnp.int32, (n, 1), 0)
-    for p in range(n):
-        row = m[p : p + 1, :]
-        col = m[:, p : p + 1]
-        r = 1.0 / jnp.broadcast_to(m[p : p + 1, p : p + 1], (1, n))
-        row = jnp.where(lane == p, r, row * r)
-        m = jnp.where(sub == p, row, jnp.where(lane == p, 0.0, m) - col * row)
+    for p in range(0, n, 2):
+        q = p + 1
+        row_p, row_q = m[p:q, :], m[q : q + 1, :]
+        col_p, col_q = m[:, p:q], m[:, q : q + 1]
+        a = jnp.broadcast_to(m[p:q, p:q], (1, n))
+        b = jnp.broadcast_to(m[p:q, q : q + 1], (1, n))
+        d = jnp.broadcast_to(m[q : q + 1, q : q + 1], (1, n))
+        r = 1.0 / (a * d - b * b)
+        a, b, d = d * r, -b * r, a * r
+        new_p = jnp.where(lane == p, a, jnp.where(lane == q, b, a * row_p + b * row_q))
+        new_q = jnp.where(lane == p, b, jnp.where(lane == q, d, b * row_p + d * row_q))
+        rest = jnp.where((lane == p) | (lane == q), 0.0, m)
+        m = jnp.where(
+            sub == p, new_p,
+            jnp.where(sub == q, new_q, rest - col_p * new_p - col_q * new_q),
+        )
     return m
 
 
@@ -429,11 +434,15 @@
 
 
 def per_device(hidden, positions, gate_weight, up_weight, inv_cov, target_res):
-    subject = jnp.take(hidden, positions, axis=0)
-    dims = (((0,), (1,)), ((), ()))
+    tokens = lax.broadcasted_iota(jnp.int32, (positions.shape[0], hidden.shape[0]), 1)
+    chosen = (positions[:, None] == tokens).astype(BF16)
+    subject = lax.dot_general(
+        hidden, chosen, (((0,), (1,)), ((), ())), preferred_element_type=F32
+    ).astype(BF16)
+    dims = (((0,), (0,)), ((), ()))
     gate = lax.dot_general(gate_weight, subject, dims, preferred_element_type=F32)
     up = lax.dot_general(up_weight, subject, dims, preferred_element_type=F32)
-    system, image_t = exchange(jnp.stack([gate, up]), inv_cov)
+    system, image_t = exchange(gate, up, inv_cov)
     return solve(system, target_res, image_t)
 
 

time: 208 us -> 181 us (0.87)
  Pallas kernels: 193 us -> 170 us
  matrix products: 2.47 us -> 8.11 us
  other arithmetic: 5.3 us -> 0 us
  local copies, waits for them, and re-layouts: 6.31 us -> 2.73 us
    pallas_call x1, Pallas kernels: 53.8 us -> 40 us  [solve(): pl.pallas_call(solve_kernel, name='solve', out_shape=jax.ShapeDtypeStruct...]
    pallas_call x1, Pallas kernels: 139 us -> 130 us  [exchange(): pl.pallas_call(exchange_kernel, name='exchange', out_shape=(jax.ShapeDtyp...]
    another operation x1 -> x0, other arithmetic: 3.79 us -> none  [per_device(): system, image_t = exchange(jnp.stack([gate, up]), inv_cov)]
    gather x1 -> x0, local copies, waits for them, and re-layouts: 3.34 us -> none  [per_device(): subject = jnp.take(hidden, positions, axis=0)]
    dot_general x0 -> x1, matrix products: none -> 2.13 us  [per_device(): lax.dot_general(hidden, chosen, (((0,), (1,)), ((), ())), preferred_eleme...]
where the time goes in v3:
time: 181 us; the launch traced here: 180 us
  Pallas kernels  170 us (94%)
  matrix products  8.11 us (4%)
  local copies, waits for them, and re-layouts  2.73 us (2%)
    pallas_call x1, Pallas kernels, exchange(): pl.pallas_call(exchange_kernel, name='exchange', out_shape=(jax.ShapeDtyp...  130 us
    pallas_call x1, Pallas kernels, solve(): pl.pallas_call(solve_kernel, name='solve', out_shape=jax.ShapeDtypeStruct...  40 us

profile of v3, /device:TPU:1, one launch (start us, length us, event | category | flops | bytes accessed | tf_op | source)
XLA Modules:
  0.0 180.4 jit_solution(16182474226506966371)
XLA Ops:
  0.0 0.0 copy-start
  0.0 2.1 %fusion.1 = bf16[512,512]{1,0:T(8,128)(2,1)S(1)} fusion(bf16[1024,512]{1,0:T(8,128)(2,1)} %param.6, s32[512]{0:T(512)} %param.7), kind=kOutput, calls=%fused_computation.4 | convolution fusion | flops 537657344 | bytes 1574912 | tf_op jit(solution)/shard_map/dot_general | solution.py:439
  2.1 0.0 copy-done
  2.1 0.0 copy-start.4
  2.2 3.0 %convolution_bitcast_fusion.up = f32[1792,512]{1,0:T(8,128)} fusion(bf16[512,512]{1,0:T(8,128)(2,1)S(1)} %fusion.1, bf16[512,1792]{1,0:T(8,128)(2,1)S(1)} %copy-done), kind=kOutput, calls=%fused_computation | convolution fusion | flops 939524096 | bytes 6029312 | tf_op jit(solution)/shard_map/dot_general | solution.py:444
  5.2 0.0 copy-done.4
  5.2 3.0 %convolution_bitcast_fusion.1.gate = f32[1792,512]{1,0:T(8,128)} fusion(bf16[512,512]{1,0:T(8,128)(2,1)S(1)} %fusion.1, bf16[512,1792]{1,0:T(8,128)(2,1)S(1)} %copy-done.4), kind=kOutput, calls=%fused_computation.1 | convolution fusion | flops 939524096 | bytes 6029312 | tf_op jit(solution)/shard_map/dot_general | solution.py:443
  8.1 0.0 copy-start.3
  8.1 129.6 %exchange.1 = (f32[512,512]{1,0:T(8,128)}, bf16[1792,512]{1,0:T(8,128)(2,1)}) custom-call(f32[1792,512]{1,0:T(8,128)} %convolution_bitcast_fusion.1.gate, f32[1792,512]{1,0:T(8,128)} %convolution_bitcast_fusion.up, bf16[1792,1792]{1,0:T(8,128)(2,1)} %cov_hbm.1), custom_call_target="tpu_custom_call" | custom-call | tf_op jit(solution)/shard_map/exchange/pallas_call | solution.py:342
  137.7 0.0 copy-done.3
  137.7 0.0 copy-start.1
  137.7 1.5 copy-done.1
  139.2 0.0 copy-start.2
  139.2 1.2 copy-done.2
  140.5 40.0 %solve.1 = bf16[512,1792]{1,0:T(8,128)(2,1)} custom-call(f32[512,512]{1,0:T(8,128)S(1)} %copy-done.2, bf16[512,512]{1,0:T(8,128)(2,1)S(1)} %copy-done.3, bf16[1792,512]{1,0:T(8,128)(2,1)S(1)} %copy-done.1), custom_call_target="tpu_custom_call" | custom-call | tf_op jit(solution)/shard_map/solve/pallas_call | solution.py:425
Async XLA Ops:
  0.0 2.1 %copy-start = (bf16[512,1792]{1,0:T(8,128)(2,1)S(1)}, bf16[512,1792]{1,0:T(8,128)(2,1)}, u32[]{:S(2)}) copy-start(bf16[512,1792]{1,0:T(8,128)(2,1)} %param.9) | copy-start | bytes 5505028
  2.1 3.0 %copy-start.4 = (bf16[512,1792]{1,0:T(8,128)(2,1)S(1)}, bf16[512,1792]{1,0:T(8,128)(2,1)}, u32[]{:S(2)}) copy-start(bf16[512,1792]{1,0:T(8,128)(2,1)} %param.8) | copy-start | bytes 5505028
  8.1 129.6 %copy-start.3 = (bf16[512,512]{1,0:T(8,128)(2,1)S(1)}, bf16[512,512]{1,0:T(8,128)(2,1)}, u32[]{:S(2)}) copy-start(bf16[512,512]{1,0:T(8,128)(2,1)} %t_ref.1) | copy-start | bytes 1572868
  137.7 1.5 copy-start.1
  139.2 1.2 copy-start.2

commit v4 on v3

--- a/solution.py
+++ b/solution.py
@@ -10,11 +10,95 @@
 BF16 = jnp.bfloat16
 
 
+def invert(m):
+    n = m.shape[0]
+    lane = lax.broadcasted_iota(jnp.int32, (1, n), 1)
+    sub = lax.broadcasted_iota(jnp.int32, (n, 1), 0)
+    for p in range(0, n, 4):
+        row = [m[p + i : p + i + 1, :] for i in range(4)]
+        col = [m[:, p + i : p + i + 1] for i in range(4)]
+
+        def at(i, j):
+            return jnp.broadcast_to(row[i][:, p + j : p + j + 1], (1, n))
+
+        a, b, d = at(0, 0), at(0, 1), at(1, 1)
+        r = 1.0 / (a * d - b * b)
+        a, b, d = d * r, -b * r, a * r
+        c = [[at(0, 2), at(0, 3)], [at(1, 2), at(1, 3)]]
+        e = [[a * c[0][j] + b * c[1][j] for j in (0, 1)],
+             [b * c[0][j] + d * c[1][j] for j in (0, 1)]]
+        s0 = at(2, 2) - (c[0][0] * e[0][0] + c[1][0] * e[1][0])
+        s1 = at(2, 3) - (c[0][0] * e[0][1] + c[1][0] * e[1][1])
+        s2 = at(3, 3) - (c[0][1] * e[0][1] + c[1][1] * e[1][1])
+        r = 1.0 / (s0 * s2 - s1 * s1)
+        s0, s1, s2 = s2 * r, -s1 * r, s0 * r
+        f = [[e[i][0] * s0 + e[i][1] * s1, e[i][0] * s1 + e[i][1] * s2] for i in (0, 1)]
+        top = [[None, None], [None, None]]
+        for i in (0, 1):
+            for j in (0, 1):
+                base = ((a, b), (b, d))[i][j]
+                top[i][j] = base + f[i][0] * e[j][0] + f[i][1] * e[j][1]
+        inv = [
+            [top[0][0], top[0][1], -f[0][0], -f[0][1]],
+            [top[1][0], top[1][1], -f[1][0], -f[1][1]],
+            [-f[0][0], -f[1][0], s0, s1],
+            [-f[0][1], -f[1][1], s1, s2],
+        ]
+        new = []
+        for i in range(4):
+            v = (inv[i][0] * row[0] + inv[i][1] * row[1]) + (
+                inv[i][2] * row[2] + inv[i][3] * row[3]
+            )
+            for j in range(4):
+                v = jnp.where(lane == p + j, inv[i][j], v)
+            new.append(v)
+        rest = jnp.where((lane >= p) & (lane < p + 4), 0.0, m)
+        m = rest - (col[0] * new[0] + col[1] * new[1]) - (
+            col[2] * new[2] + col[3] * new[3]
+        )
+        for i in range(4):
+            m = jnp.where(sub == p + i, new[i], m)
+    return m
+
+
+def right_solve(system, a, target, between):
+    n = a.shape[0]
+    b = n // 4
+    eye = lax.broadcasted_iota(jnp.int32, (n, n), 0) == lax.broadcasted_iota(
+        jnp.int32, (n, n), 1
+    )
+    a[...] = system[...] + jnp.where(eye, 1.0, 0.0)
+
+    def dot(p, q):
+        return jnp.dot(p, q, precision=lax.Precision.HIGHEST, preferred_element_type=F32)
+
+    def block(k, carry):
+        pl.when(k == 2)(between)
+        d = pl.ds(pl.multiple_of(k * b, b), b)
+        inv = invert(a[d, d])
+        col = a[:, d]
+        wide = dot(inv, a[d, :])
+        a[...] = a[...] - dot(col, wide)
+        a[:, d] = -dot(col, inv)
+        a[d, :] = wide
+        a[d, d] = inv
+        return carry
+
+    lax.fori_loop(0, 4, block, 0)
+    v = a[...]
+    coeffs = jnp.zeros((target.shape[0], n), F32)
+    for _ in range(3):
+        short = v.astype(BF16)
+        coeffs = coeffs + jnp.dot(target[...], short, preferred_element_type=F32)
+        v = v - short.astype(F32)
+    return coeffs.astype(BF16)
+
+
 def exchange_kernel(
-    gate, up, cov_hbm, s_out, img_out,
-    cov, ysend, yrecv, psend, precv, qsend, qrecv, qy_s, qy_r,
+    subject, target, gate_hbm, up_hbm, cov_hbm, coeffs_out, img_out, s_out, work,
+    weights, proj, cov, ysend, yrecv, psend, precv, qsend, qrecv, qy_s, qy_r,
     kt, kts, cxs, cxr, cs, cr, spart, exs, exr, e1s, e1r, e2s, e2r, e3, s2,
-    cov_sem, y_ss, y_rs, z_ss, z_rs, qy_ss, qy_rs, b_ss, b_rs, t_ss, t_rs,
+    w_sem, cov_sem, y_ss, y_rs, z_ss, z_rs, qy_ss, qy_rs, b_ss, b_rs, t_ss, t_rs,
     cx_ss, cx_rs, c_ss, c_rs, ex_ss, ex_rs, e1_ss, e1_rs, e2_ss, e2_rs,
     e3_ss, e3_rs, e4_ss, e4_rs, d_ss, d_rs, loc_sem,
 ):
@@ -47,10 +131,15 @@
     t_out = (me_c, ((me_r % 8 + 4) % 8) * 2 + me_r // 8)
     t_in = (own_sub, me_r)
 
+    loads = [
+        pltpu.make_async_copy(gate_hbm, weights.at[0], w_sem.at[0]),
+        pltpu.make_async_copy(up_hbm, weights.at[1], w_sem.at[1]),
+    ]
     cov_copy = pltpu.make_async_copy(cov_hbm, cov, cov_sem)
-    cov_copy.start()
+    for cp in loads + [cov_copy]:
+        cp.start()
+
     kts[...] = jnp.zeros_like(kts)
-
     barrier = pltpu.get_barrier_semaphore()
     peers = [((me_r + k) % 16, me_c) for k in range(1, 16)]
     peers += [g_to(k) for k in range(1, 8)] + [partner, t_out, t_in]
@@ -58,9 +147,25 @@
         pl.semaphore_signal(barrier, inc=1, device_id=p, device_id_type=MESH)
     lo, hi = pl.ds(0, half), pl.ds(half, half)
     pending = []
+    width = proj.shape[1] // 7
+
+    def project(i):
+        def step(j, carry):
+            at = pl.ds(pl.multiple_of(j * width, width), width)
+            proj[i, at, :] = lax.dot_general(
+                weights[i, :, at], subject[...], (((0,), (0,)), ((), ())),
+                preferred_element_type=F32,
+            )
+            return carry
+
+        loads[i].wait()
+        lax.fori_loop(0, 7, step, 0)
+
+    project(0)
+    project(1)
 
     def projections(r, lanes):
-        return jnp.stack([gate[rows(r), lanes], up[rows(r), lanes]])
+        return proj[:, rows(r), lanes]
 
     order = (4, 3, 5, 2, 6, 1, 7, 0)
     for o in order:
@@ -147,8 +252,6 @@
         forward(0, side, 1, 0)
         forward(1, side, 1, 0)
     across(0, 0)
-    tr = send(mine, kts.at[pl.ds(0, ch)], t_ss, t_rs, *t_out)
-    tr.start()
     bc["y"].wait_recv()
     for side in (0, 1):
         forward(0, side, 1, 1)
@@ -165,6 +268,8 @@
     for key in list(bc):
         if key != "y" and key[0] == "y":
             bc[key].wait_recv()
+    tr = send(mine, kts.at[pl.ds(0, ch)], t_ss, t_rs, *t_out)
+    tr.start()
     pending += [tr] + list(bc.values())
 
     cov_copy.wait()
@@ -258,7 +363,6 @@
     def s_ref(gg):
         return s_out.at[rows(core * 8 + gg, blk)]
 
-    gather(img_ref, d_ss, d_rs, dc)
     v = e1s[rows(g, blk), :]
     for k in range(1, 8):
         e1c[k - 1].wait_recv()
@@ -300,11 +404,24 @@
     ec = {}
     gather(s_ref, e4_ss, e4_rs, ec)
     relay(s_ref, e4_ss, e4_rs, ec)
-    relay(img_ref, d_ss, d_rs, dc)
-    for out in (ec, dc):
-        out[0].wait_recv()
+    gather(img_ref, d_ss, d_rs, dc)
+    ec[0].wait_recv()
+    for k in range(1, 8):
+        ec[7 + k].wait_recv()
+
+    def d_relay(k):
+        ref = img_ref((g - k + 8) % 8)
+        return send(ref, ref, d_ss.at[7 + k], d_rs.at[7 + k], *partner)
+
+    def relay_images():
         for k in range(1, 8):
-            out[7 + k].wait_recv()
+            dc[k].wait_recv()
+            d_relay(k).start()
+
+    coeffs_out[...] = right_solve(s_out, work, target, relay_images)
+    dc[0].wait_recv()
+    for k in range(1, 8):
+        d_relay(k).wait()
     pending += [ex] + e1c + e2c + e3c + list(ec.values()) + list(dc.values())
     for cp in pending:
         cp.wait_send()
@@ -314,13 +431,14 @@
         c_copy(k).wait_send()
 
 
-def exchange(gate, up, inv_cov):
-    ff, facts = gate.shape
+def exchange(subject, target, gate_weight, up_weight, inv_cov):
+    ff, facts = gate_weight.shape[1], subject.shape[1]
     ch, half, blk = ff // 16, facts // 2, facts // 16
     dma = pltpu.SemaphoreType.DMA
     vm = pltpu.VMEM
     scratch = [
-        vm(inv_cov.shape, BF16),
+        vm((facts, facts), F32), vm((facts, facts), F32), vm((2,) + gate_weight.shape, BF16),
+        vm((2, ff, facts), F32), vm(inv_cov.shape, BF16),
         vm((8, 2, ch, half), BF16), vm((8, 2, ch, half), BF16),
         vm((7, 2, ch, half), BF16), vm((7, 2, ch, half), BF16),
         vm((7, 2, 2, ch, half), BF16), vm((7, 2, 2, ch, half), BF16),
@@ -333,7 +451,7 @@
         vm((facts // 2, facts), F32), vm((8, blk, facts), BF16),
         vm((8, blk, facts), BF16), vm((16, 8, 128), F32), vm((8, 128), F32),
         vm((blk, facts), F32),
-        dma(()), dma((8,)), dma((8,)), dma((24,)), dma((24,)), dma(()), dma(()),
+        dma((2,)), dma(()), dma((8,)), dma((8,)), dma((24,)), dma((24,)), dma(()), dma(()),
         dma((41,)), dma((41,)), dma(()), dma(()),
         dma((8,)), dma((8,)), dma((8,)), dma((8,)), dma(()), dma(()),
         dma((8,)), dma((8,)), dma((16,)), dma((16,)), dma((16,)), dma((16,)),
@@ -343,12 +461,14 @@
         exchange_kernel,
         name="exchange",
         out_shape=(
-            jax.ShapeDtypeStruct((facts, facts), F32),
+            jax.ShapeDtypeStruct(target.shape, BF16),
             jax.ShapeDtypeStruct((ff, facts), BF16),
         ),
         in_specs=[
             pl.BlockSpec(memory_space=pltpu.VMEM),
             pl.BlockSpec(memory_space=pltpu.VMEM),
+            pl.BlockSpec(memory_space=pl.ANY),
+            pl.BlockSpec(memory_space=pl.ANY),
             pl.BlockSpec(memory_space=pl.ANY),
         ],
         out_specs=[pl.BlockSpec(memory_space=pltpu.VMEM)] * 2,
@@ -356,81 +476,7 @@
         compiler_params=pltpu.CompilerParams(
             collective_id=0, has_side_effects=True, vmem_limit_bytes=60 * 2**20
         ),
-    )(gate, up, inv_cov)
-
-
-def invert(m):
-    n = m.shape[0]
-    lane = lax.broadcasted_iota(jnp.int32, (1, n), 1)
-    sub = lax.broadcasted_iota(jnp.int32, (n, 1), 0)
-    for p in range(0, n, 2):
-        q = p + 1
-        row_p, row_q = m[p:q, :], m[q : q + 1, :]
-        col_p, col_q = m[:, p:q], m[:, q : q + 1]
-        a = jnp.broadcast_to(m[p:q, p:q], (1, n))
-        b = jnp.broadcast_to(m[p:q, q : q + 1], (1, n))
-        d = jnp.broadcast_to(m[q : q + 1, q : q + 1], (1, n))
-        r = 1.0 / (a * d - b * b)
-        a, b, d = d * r, -b * r, a * r
-        new_p = jnp.where(lane == p, a, jnp.where(lane == q, b, a * row_p + b * row_q))
-        new_q = jnp.where(lane == p, b, jnp.where(lane == q, d, b * row_p + d * row_q))
-        rest = jnp.where((lane == p) | (lane == q), 0.0, m)
-        m = jnp.where(
-            sub == p, new_p,
-            jnp.where(sub == q, new_q, rest - col_p * new_p - col_q * new_q),
-        )
-    return m
-
-
-def solve_kernel(s_ref, t_ref, img_ref, out_ref, a):
-    n = s_ref.shape[0]
-    b = min(128, n)
-    eye = lax.broadcasted_iota(jnp.int32, (n, n), 0) == lax.broadcasted_iota(
-        jnp.int32, (n, n), 1
-    )
-    a[...] = s_ref[...] + jnp.where(eye, 1.0, 0.0)
-
-    def dot(p, q):
-        return jnp.dot(p, q, precision=lax.Precision.HIGHEST, preferred_element_type=F32)
-
-    def block(k, carry):
-        d = pl.ds(pl.multiple_of(k * b, b), b)
-        inv = invert(a[d, d])
-        col = a[:, d]
-        wide = dot(inv, a[d, :])
-        a[...] = a[...] - dot(col, wide)
-        a[:, d] = -dot(col, inv)
-        a[d, :] = wide
-        a[d, d] = inv
-        return carry
-
-    lax.fori_loop(0, n // b, block, 0)
-    v = a[...]
-    coeffs = jnp.zeros((t_ref.shape[0], n), F32)
-    for _ in range(3):
-        short = v.astype(BF16)
-        coeffs = coeffs + jnp.dot(t_ref[...], short, preferred_element_type=F32)
-        v = v - short.astype(F32)
-    coeffs = coeffs.astype(BF16)
-    w = 256
-    for j in range(out_ref.shape[1] // w):
-        out_ref[:, j * w : (j + 1) * w] = lax.dot_general(
-            coeffs, img_ref[j * w : (j + 1) * w, :], (((1,), (1,)), ((), ())),
-            preferred_element_type=F32,
-        ).astype(BF16)
-
-
-def solve(system, target, image_t):
-    n = system.shape[0]
-    return pl.pallas_call(
-        solve_kernel,
-        name="solve",
-        out_shape=jax.ShapeDtypeStruct((target.shape[0], image_t.shape[0]), BF16),
-        in_specs=[pl.BlockSpec(memory_space=pltpu.VMEM)] * 3,
-        out_specs=pl.BlockSpec(memory_space=pltpu.VMEM),
-        scratch_shapes=[pltpu.VMEM((n, n), F32)],
-        compiler_params=pltpu.CompilerParams(vmem_limit_bytes=40 * 2**20),
-    )(system, target, image_t)
+    )(subject, target, gate_weight, up_weight, inv_cov)
 
 
 def per_device(hidden, positions, gate_weight, up_weight, inv_cov, target_res):
@@ -439,11 +485,10 @@
     subject = lax.dot_general(
         hidden, chosen, (((0,), (1,)), ((), ())), preferred_element_type=F32
     ).astype(BF16)
-    dims = (((0,), (0,)), ((), ()))
-    gate = lax.dot_general(gate_weight, subject, dims, preferred_element_type=F32)
-    up = lax.dot_general(up_weight, subject, dims, preferred_element_type=F32)
-    system, image_t = exchange(gate, up, inv_cov)
-    return solve(system, target_res, image_t)
+    coeffs, image_t = exchange(subject, target_res, gate_weight, up_weight, inv_cov)
+    return lax.dot_general(
+        coeffs, image_t, (((1,), (1,)), ((), ())), preferred_element_type=F32
+    ).astype(BF16)
 
 
 def solution(mesh):

time: 181 us -> 168 us (0.928)
  Pallas kernels: 170 us -> 160 us
    pallas_call x1 -> x0, Pallas kernels: 40 us -> none  [solve(): pl.pallas_call(solve_kernel, name='solve', out_shape=jax.ShapeDtypeStruct...]
    pallas_call x1, Pallas kernels: 130 us -> 160 us  [exchange(): pl.pallas_call(exchange_kernel, name='exchange', out_shape=(jax.ShapeDtyp...]
    dot_general x2 -> x1, matrix products: 5.98 us -> 4.07 us  [per_device(): lax.dot_general(coeffs, image_t, (((1,), (1,)), ((), ())), preferred_elem...]
where the time goes in v4:
time: 168 us
  Pallas kernels  160 us (95%)
  matrix products  6.42 us (4%)
    pallas_call x1, Pallas kernels, exchange(): pl.pallas_call(exchange_kernel, name='exchange', out_shape=(jax.ShapeDtyp...  160 us
    dot_general x1, matrix products, per_device(): lax.dot_general(coeffs, image_t, (((1,), (1,)), ((), ())), preferred_elem...  4.07 us

profile of v4, /device:TPU:1, one launch (start us, length us, event | category | flops | bytes accessed | tf_op | source)
XLA Modules:
  0.0 167.7 jit_solution(14711923041513336677)
XLA Ops:
  0.0 0.0 copy-start
  0.0 1.2 copy-done
  1.2 2.4 %fusion.2.subject = bf16[512,512]{1,0:T(8,128)(2,1)} fusion(bf16[1024,512]{1,0:T(8,128)(2,1)S(1)} %copy-done, s32[512]{0:T(512)} %param.7), kind=kOutput, calls=%fused_computation.4 | convolution fusion | flops 537657344 | bytes 1574912 | tf_op jit(solution)/shard_map/dot_general | solution.py:485
  3.6 160.0 %exchange.1 = (bf16[512,512]{1,0:T(8,128)(2,1)}, bf16[1792,512]{1,0:T(8,128)(2,1)}) custom-call(bf16[512,512]{1,0:T(8,128)(2,1)} %fusion.2.subject, bf16[512,512]{1,0:T(8,128)(2,1)} %target.1, bf16[512,1792]{1,0:T(8,128)(2,1)} %gate_hbm.1, bf16[512,1792]{1,0:T(8,128)(2,1)} %up_hbm.1, bf16[1792,1792]{1,0:T(8,128)(2,1)} %cov_hbm.1), custom_call_target="tpu_custom_call" | custom-call | tf_op jit(solution)/shard_map/exchange/pallas_call | solution.py:460
  163.6 4.1 %convolution_convert_fusion = bf16[512,1792]{1,0:T(8,128)(2,1)} fusion(bf16[512,512]{1,0:T(8,128)(2,1)} %get-tuple-element.7, bf16[1792,512]{1,0:T(8,128)(2,1)} %get-tuple-element.8), kind=kOutput, calls=%fused_computation | convolution fusion | flops 940441600 | bytes 4194304 | tf_op jit(solution)/shard_map/dot_general | solution.py:489
Async XLA Ops:
  0.0 1.2 copy-start

commit v5 on v4

--- a/solution.py
+++ b/solution.py
@@ -61,7 +61,7 @@
     return m
 
 
-def right_solve(system, a, target, between):
+def right_solve(system, a, pivot, target, between):
     n = a.shape[0]
     b = n // 4
     eye = lax.broadcasted_iota(jnp.int32, (n, n), 0) == lax.broadcasted_iota(
@@ -75,7 +75,11 @@
     def block(k, carry):
         pl.when(k == 2)(between)
         d = pl.ds(pl.multiple_of(k * b, b), b)
-        inv = invert(a[d, d])
+        @pl.when(k < 4)
+        def _():
+            pivot[...] = invert(a[d, d])
+
+        inv = pivot[...]
         col = a[:, d]
         wide = dot(inv, a[d, :])
         a[...] = a[...] - dot(col, wide)
@@ -95,9 +99,9 @@
 
 
 def exchange_kernel(
-    subject, target, gate_hbm, up_hbm, cov_hbm, coeffs_out, img_out, s_out, work,
+    subject, target, gate_hbm, up_hbm, cov_hbm, coeffs_out, img_out, s_out, work, pivot,
     weights, proj, cov, ysend, yrecv, psend, precv, qsend, qrecv, qy_s, qy_r,
-    kt, kts, cxs, cxr, cs, cr, spart, exs, exr, e1s, e1r, e2s, e2r, e3, s2,
+    kt, kts, cxs, cxr, cs, cr, exs, exr, e1s, e1r, e2s, e2r, e3, s2,
     w_sem, cov_sem, y_ss, y_rs, z_ss, z_rs, qy_ss, qy_rs, b_ss, b_rs, t_ss, t_rs,
     cx_ss, cx_rs, c_ss, c_rs, ex_ss, ex_rs, e1_ss, e1_rs, e2_ss, e2_rs,
     e3_ss, e3_rs, e4_ss, e4_rs, d_ss, d_rs, loc_sem,
@@ -136,7 +140,7 @@
         pltpu.make_async_copy(up_hbm, weights.at[1], w_sem.at[1]),
     ]
     cov_copy = pltpu.make_async_copy(cov_hbm, cov, cov_sem)
-    for cp in loads + [cov_copy]:
+    for cp in loads:
         cp.start()
 
     kts[...] = jnp.zeros_like(kts)
@@ -162,6 +166,7 @@
         lax.fori_loop(0, 7, step, 0)
 
     project(0)
+    cov_copy.start()
     project(1)
 
     def projections(r, lanes):
@@ -317,20 +322,22 @@
 
     tr.wait_recv()
     pad = jnp.zeros((kts.shape[0] - ch, kts.shape[1]), BF16)
-    dims = (((0,), (0,)), ((), ()))
-    keys_s = kts[...]
-    part = lax.dot_general(
-        keys_s, jnp.concatenate([v_hi, pad], 0), dims, preferred_element_type=F32
-    ) + lax.dot_general(
-        keys_s, jnp.concatenate([v_lo, pad], 0), dims, preferred_element_type=F32
-    )
-    spart[...] = part
-    n2 = spart.shape[0] // 2
-    exs[...] = spart[rows(1 - core, n2), :].astype(BF16)
+    image_s = jnp.concatenate([v_hi, pad, v_lo, pad], 0)
+    n2 = kts.shape[1] // 2
+
+    def system_half(i):
+        keys_s = kts[:, pl.ds(pl.multiple_of(i * n2, n2), n2)]
+        return lax.dot_general(
+            jnp.concatenate([keys_s, keys_s], 0), image_s, (((0,), (0,)), ((), ())),
+            preferred_element_type=F32,
+        )
+
+    exs[...] = system_half(1 - core).astype(BF16)
     ex = send(exs, exr, ex_ss, ex_rs, *partner)
     ex.start()
+    own_half = system_half(core)
     ex.wait_recv()
-    e1s[...] = (spart[rows(core, n2), :] + exr[...].astype(F32))
+    e1s[...] = own_half + exr[...].astype(F32)
     blk = n2 // 8
     e1c = []
     for k in range(1, 8):
@@ -418,7 +425,7 @@
             dc[k].wait_recv()
             d_relay(k).start()
 
-    coeffs_out[...] = right_solve(s_out, work, target, relay_images)
+    coeffs_out[...] = right_solve(s_out, work, pivot, target, relay_images)
     dc[0].wait_recv()
     for k in range(1, 8):
         d_relay(k).wait()
@@ -437,7 +444,8 @@
     dma = pltpu.SemaphoreType.DMA
     vm = pltpu.VMEM
     scratch = [
-        vm((facts, facts), F32), vm((facts, facts), F32), vm((2,) + gate_weight.shape, BF16),
+        vm((facts, facts), F32), vm((facts, facts), F32),
+        vm((facts // 4, facts // 4), F32), vm((2,) + gate_weight.shape, BF16),
         vm((2, ff, facts), F32), vm(inv_cov.shape, BF16),
         vm((8, 2, ch, half), BF16), vm((8, 2, ch, half), BF16),
         vm((7, 2, ch, half), BF16), vm((7, 2, ch, half), BF16),
@@ -446,7 +454,6 @@
         vm((ff, facts), BF16), vm((-(-ch // 128) * 128, facts), BF16),
         vm((8, ch, facts), BF16), vm((8, ch, facts), BF16),
         vm((8, ch, facts), BF16), vm((8, ch, facts), BF16),
-        vm((facts, facts), F32),
         vm((facts // 2, facts), BF16), vm((facts // 2, facts), BF16),
         vm((facts // 2, facts), F32), vm((8, blk, facts), BF16),
         vm((8, blk, facts), BF16), vm((16, 8, 128), F32), vm((8, 128), F32),

time: 168 us -> 153 us (0.911)
  Pallas kernels: 160 us -> 145 us
    pallas_call x1, Pallas kernels: 160 us -> 145 us  [exchange(): pl.pallas_call(exchange_kernel, name='exchange', out_shape=(jax.ShapeDtyp...]
where the time goes in v5:
time: 153 us
  Pallas kernels  145 us (95%)
  matrix products  6.41 us (4%)
    pallas_call x1, Pallas kernels, exchange(): pl.pallas_call(exchange_kernel, name='exchange', out_shape=(jax.ShapeDtyp...  145 us
    dot_general x1, matrix products, per_device(): lax.dot_general(coeffs, image_t, (((1,), (1,)), ((), ())), preferred_elem...  4.05 us

profile of v5, /device:TPU:1, one launch (start us, length us, event | category | flops | bytes accessed | tf_op | source)
XLA Modules:
  0.0 152.6 jit_solution(5793783567469765762)
XLA Ops:
  0.0 0.0 copy-start
  0.0 1.2 copy-done
  1.2 2.4 %fusion.2.subject = bf16[512,512]{1,0:T(8,128)(2,1)} fusion(bf16[1024,512]{1,0:T(8,128)(2,1)S(1)} %copy-done, s32[512]{0:T(512)} %param.7), kind=kOutput, calls=%fused_computation.4 | convolution fusion | flops 537657344 | bytes 1574912 | tf_op jit(solution)/shard_map/dot_general | solution.py:492
  3.6 145.0 %exchange.1 = (bf16[512,512]{1,0:T(8,128)(2,1)}, bf16[1792,512]{1,0:T(8,128)(2,1)}) custom-call(bf16[512,512]{1,0:T(8,128)(2,1)} %fusion.2.subject, bf16[512,512]{1,0:T(8,128)(2,1)} %target.1, bf16[512,1792]{1,0:T(8,128)(2,1)} %gate_hbm.1, bf16[512,1792]{1,0:T(8,128)(2,1)} %up_hbm.1, bf16[1792,1792]{1,0:T(8,128)(2,1)} %cov_hbm.1), custom_call_target="tpu_custom_call" | custom-call | tf_op jit(solution)/shard_map/exchange/pallas_call | solution.py:467
  148.5 4.1 %convolution_convert_fusion = bf16[512,1792]{1,0:T(8,128)(2,1)} fusion(bf16[512,512]{1,0:T(8,128)(2,1)} %get-tuple-element.7, bf16[1792,512]{1,0:T(8,128)(2,1)} %get-tuple-element.8), kind=kOutput, calls=%fused_computation | convolution fusion | flops 940441600 | bytes 4194304 | tf_op jit(solution)/shard_map/dot_general | solution.py:496
Async XLA Ops:
  0.0 1.2 copy-start

commit v6 on v5

--- a/solution.py
+++ b/solution.py
@@ -13,7 +13,7 @@
 def invert(m):
     n = m.shape[0]
     lane = lax.broadcasted_iota(jnp.int32, (1, n), 1)
-    sub = lax.broadcasted_iota(jnp.int32, (n, 1), 0)
+    sub = lax.broadcasted_iota(jnp.int32, (8, 1), 0)
     for p in range(0, n, 4):
         row = [m[p + i : p + i + 1, :] for i in range(4)]
         col = [m[:, p + i : p + i + 1] for i in range(4)]
@@ -56,8 +56,12 @@
         m = rest - (col[0] * new[0] + col[1] * new[1]) - (
             col[2] * new[2] + col[3] * new[3]
         )
+        g0 = p // 8 * 8
+        group = m[g0 : g0 + 8, :]
         for i in range(4):
-            m = jnp.where(sub == p + i, new[i], m)
+            group = jnp.where(sub == p + i - g0, new[i], group)
+        parts = [m[:g0, :]] * (g0 > 0) + [group] + [m[g0 + 8 :, :]] * (g0 + 8 < n)
+        m = jnp.concatenate(parts, 0)
     return m
 
 
@@ -99,8 +103,8 @@
 
 
 def exchange_kernel(
-    subject, target, gate_hbm, up_hbm, cov_hbm, coeffs_out, img_out, s_out, work, pivot,
-    weights, proj, cov, ysend, yrecv, psend, precv, qsend, qrecv, qy_s, qy_r,
+    subject, target_hbm, gate_hbm, up_hbm, cov_hbm, coeffs_out, img_out, s_out, work, pivot,
+    target, weights, proj, cov, ysend, yrecv, psend, precv, qsend, qrecv, qy_s, qy_r,
     kt, kts, cxs, cxr, cs, cr, exs, exr, e1s, e1r, e2s, e2r, e3, s2,
     w_sem, cov_sem, y_ss, y_rs, z_ss, z_rs, qy_ss, qy_rs, b_ss, b_rs, t_ss, t_rs,
     cx_ss, cx_rs, c_ss, c_rs, ex_ss, ex_rs, e1_ss, e1_rs, e2_ss, e2_rs,
@@ -140,6 +144,7 @@
         pltpu.make_async_copy(up_hbm, weights.at[1], w_sem.at[1]),
     ]
     cov_copy = pltpu.make_async_copy(cov_hbm, cov, cov_sem)
+    target_copy = pltpu.make_async_copy(target_hbm, target, w_sem.at[2])
     for cp in loads:
         cp.start()
 
@@ -167,6 +172,7 @@
 
     project(0)
     cov_copy.start()
+    target_copy.start()
     project(1)
 
     def projections(r, lanes):
@@ -425,6 +431,7 @@
             dc[k].wait_recv()
             d_relay(k).start()
 
+    target_copy.wait()
     coeffs_out[...] = right_solve(s_out, work, pivot, target, relay_images)
     dc[0].wait_recv()
     for k in range(1, 8):
@@ -445,7 +452,7 @@
     vm = pltpu.VMEM
     scratch = [
         vm((facts, facts), F32), vm((facts, facts), F32),
-        vm((facts // 4, facts // 4), F32), vm((2,) + gate_weight.shape, BF16),
+        vm((facts // 4, facts // 4), F32), vm(target.shape, BF16), vm((2,) + gate_weight.shape, BF16),
         vm((2, ff, facts), F32), vm(inv_cov.shape, BF16),
         vm((8, 2, ch, half), BF16), vm((8, 2, ch, half), BF16),
         vm((7, 2, ch, half), BF16), vm((7, 2, ch, half), BF16),
@@ -458,7 +465,7 @@
         vm((facts // 2, facts), F32), vm((8, blk, facts), BF16),
         vm((8, blk, facts), BF16), vm((16, 8, 128), F32), vm((8, 128), F32),
         vm((blk, facts), F32),
-        dma((2,)), dma(()), dma((8,)), dma((8,)), dma((24,)), dma((24,)), dma(()), dma(()),
+        dma((3,)), dma(()), dma((8,)), dma((8,)), dma((24,)), dma((24,)), dma(()), dma(()),
         dma((41,)), dma((41,)), dma(()), dma(()),
         dma((8,)), dma((8,)), dma((8,)), dma((8,)), dma(()), dma(()),
         dma((8,)), dma((8,)), dma((16,)), dma((16,)), dma((16,)), dma((16,)),
@@ -473,7 +480,7 @@
         ),
         in_specs=[
             pl.BlockSpec(memory_space=pltpu.VMEM),
-            pl.BlockSpec(memory_space=pltpu.VMEM),
+            pl.BlockSpec(memory_space=pl.ANY),
             pl.BlockSpec(memory_space=pl.ANY),
             pl.BlockSpec(memory_space=pl.ANY),
             pl.BlockSpec(memory_space=pl.ANY),

time: 153 us -> 152 us (level)
  no operation moved by 1% of the time
where the time goes in v6:
time: 152 us
  Pallas kernels  145 us (95%)
  matrix products  6.41 us (4%)
    pallas_call x1, Pallas kernels, exchange(): pl.pallas_call(exchange_kernel, name='exchange', out_shape=(jax.ShapeDtyp...  145 us
    dot_general x1, matrix products, per_device(): lax.dot_general(coeffs, image_t, (((1,), (1,)), ((), ())), preferred_elem...  4.05 us

profile of v6, /device:TPU:1, one launch (start us, length us, event | category | flops | bytes accessed | tf_op | source)
XLA Modules:
  0.0 152.3 jit_solution(15398536525737616717)
XLA Ops:
  0.0 0.0 copy-start
  0.0 1.2 copy-done
  1.2 2.4 %fusion.2.subject = bf16[512,512]{1,0:T(8,128)(2,1)} fusion(bf16[1024,512]{1,0:T(8,128)(2,1)S(1)} %copy-done, s32[512]{0:T(512)} %param.7), kind=kOutput, calls=%fused_computation.4 | convolution fusion | flops 537657344 | bytes 1574912 | tf_op jit(solution)/shard_map/dot_general | solution.py:499
  3.6 144.6 %exchange.1 = (bf16[512,512]{1,0:T(8,128)(2,1)}, bf16[1792,512]{1,0:T(8,128)(2,1)}) custom-call(bf16[512,512]{1,0:T(8,128)(2,1)} %fusion.2.subject, bf16[512,512]{1,0:T(8,128)(2,1)} %target_hbm.1, bf16[512,1792]{1,0:T(8,128)(2,1)} %gate_hbm.1, bf16[512,1792]{1,0:T(8,128)(2,1)} %up_hbm.1, bf16[1792,1792]{1,0:T(8,128)(2,1)} %cov_hbm.1), custom_call_target="tpu_custom_call" | custom-call | tf_op jit(solution)/shard_map/exchange/pallas_call | solution.py:474
  148.2 4.1 %convolution_convert_fusion = bf16[512,1792]{1,0:T(8,128)(2,1)} fusion(bf16[512,512]{1,0:T(8,128)(2,1)} %get-tuple-element.7, bf16[1792,512]{1,0:T(8,128)(2,1)} %get-tuple-element.8), kind=kOutput, calls=%fused_computation | convolution fusion | flops 940441600 | bytes 4194304 | tf_op jit(solution)/shard_map/dot_general | solution.py:503
Async XLA Ops:
  0.0 1.2 copy-start
